TPU v7x, 512 devices: a whole 4x8x8 slice. The times are simulated.
512 devices in a mesh: gx: 16 (over z, core), gy: 32 (over x, y).
Axes of the slice: x: 4, y: 8, z: 8, core: 2. Of those that a mesh axis runs over, the one named last changes fastest.
Arguments:
- right_side: float32 [2, 2048, 4096], P(None, 'gx', 'gy'), may hold values from -6 to 6
- shift_coef: float32 [2048, 4096], P('gx', 'gy'), may hold values from 0.0001 to 0.001
- viscosity: float32 [2048, 4096], P('gx', 'gy'), may hold values from 1 to 10
- wet_tiles: int32 [16, 32], P('gx', 'gy'), may hold values from 0 to 1, as said below
Outputs:
- velocity: float32 [2, 2048, 4096], P(None, 'gx', 'gy')
Inputs may be any that keep to these rules, and one draw needn't show every extreme that they name: `wet_tiles`: 1 marks a wet tile of 128 x 128 cells, 0 a dry one.
All inputs are finite; a program needn't handle non-finite values.
Results may differ from a plain program's by a relative error of at most 0.00002.
Values sent between devices are 32-bit elements; how exact they have to be, the bound alone decides.
A program may use at most 64 MiB of HBM per device.

v0:
```python
import jax
import jax.numpy as jnp
from jax import lax
from jax.sharding import PartitionSpec as P

TILE = 128
LOCAL = 4
COARSE = 4
COARSE_SWEEPS = 8


OMEGA = 0.8


def extended(array, sides, width):
    for axis, dim in sides:
        devices, length = (lax.axis_size(axis), array.shape[dim])
        up = [(i, (i + 1) % devices) for i in range(devices - 1)]
        down = [(j, i) for i, j in up]
        last = lax.slice_in_dim(array, length - width, length, axis=dim)
        leading = lax.slice_in_dim(array, 0, width, axis=dim)
        before = lax.ppermute(last, axis, up)
        after = lax.ppermute(leading, axis, down)
        array = jnp.concatenate([before, array, after], axis=dim)
    return array


def swapped(block, axis, bit):
    count = lax.axis_size(axis)
    route = []
    for low in range(count):
        high = low | 1 << bit
        if high != low and high < count:
            route += [(low, high), (high, low)]
    return lax.ppermute(block, axis, route)


def pad_last(field):
    return jnp.pad(field, [(0, 0)] * (field.ndim - 2) + [(1, 1), (1, 1)])


def face_coefs(padded):
    inner = padded[1:-1, 1:-1]
    return jnp.stack(
        [
            jnp.minimum(inner, padded[:-2, 1:-1]),
            jnp.minimum(inner, padded[2:, 1:-1]),
            jnp.minimum(inner, padded[1:-1, :-2]),
            jnp.minimum(inner, padded[1:-1, 2:]),
        ]
    )


def apply_padded(padded, conduct, reaction, spacing):
    inner = padded[:, 1:-1, 1:-1]
    outflow = conduct[0] * (inner - padded[:, :-2, 1:-1]) + conduct[1] * (
        inner - padded[:, 2:, 1:-1]
    )
    outflow = (
        outflow
        + conduct[2] * (inner - padded[:, 1:-1, :-2])
        + conduct[3] * (inner - padded[:, 1:-1, 2:])
    )
    return reaction * inner + spacing * outflow


def shrink(field):
    size_x, size_y = field.shape[-2:]
    blocks = field.reshape(field.shape[:-2] + (size_x // 2, 2, size_y // 2, 2))
    return jnp.mean(blocks, axis=(-3, -1))


def widen(field):
    return jnp.repeat(jnp.repeat(field, 2, axis=-2), 2, axis=-1)


def level_solve(grid_level, source, reaction, viscous):
    conduct = face_coefs(pad_last(viscous))
    spacing = 0.25**grid_level
    diagonal = reaction + spacing * jnp.sum(conduct, axis=0)
    if grid_level == LOCAL + COARSE:
        iterate = jnp.zeros_like(source)
        for sweep_index in range(COARSE_SWEEPS):
            iterate = (
                iterate
                + OMEGA
                * (source - apply_padded(pad_last(iterate), conduct, reaction, spacing))
                / diagonal
            )
        return iterate
    iterate = OMEGA * source / diagonal
    residual = source - apply_padded(pad_last(iterate), conduct, reaction, spacing)
    correction = level_solve(grid_level + 1, shrink(residual), shrink(reaction), shrink(viscous))
    iterate = iterate + widen(correction)
    return (
        iterate
        + OMEGA * (source - apply_padded(pad_last(iterate), conduct, reaction, spacing)) / diagonal
    )


def operate(iterate, conduct, reaction, spacing):
    padded = extended(iterate, (("gx", 1), ("gy", 2)), 1)
    return apply_padded(padded, conduct, reaction, spacing)


def pair_rows(stacked, bit_index):
    partner = swapped(stacked, "gx", bit_index)
    is_upper = lax.axis_index("gx") // 2**bit_index % 2 == 1
    lower_part = jnp.where(is_upper, partner, stacked)
    upper_part = jnp.where(is_upper, stacked, partner)
    return jnp.concatenate([lower_part, upper_part], 1)


def pair_cols(stacked, bit_index):
    partner = swapped(stacked, "gy", bit_index)
    is_upper = lax.axis_index("gy") // 2**bit_index % 2 == 1
    lower_part = jnp.where(is_upper, partner, stacked)
    upper_part = jnp.where(is_upper, stacked, partner)
    return jnp.concatenate([lower_part, upper_part], 2)


def per_device(right_side, shift_coef, viscosity, wet_tiles):
    wetness = jnp.repeat(jnp.repeat(wet_tiles, TILE, axis=0), TILE, axis=1).astype(jnp.float32)
    source = right_side * wetness
    reaction = shift_coef
    viscous = viscosity * wetness
    stored = []
    for grid_level in range(LOCAL):
        padded = extended(viscous[None], (("gx", 1), ("gy", 2)), 1)[0]
        conduct = face_coefs(padded)
        spacing = 0.25**grid_level
        diagonal = reaction + spacing * jnp.sum(conduct, axis=0)
        iterate = OMEGA * source / diagonal
        residual = source - operate(iterate, conduct, reaction, spacing)
        stored.append((source, iterate, conduct, reaction, spacing, diagonal))
        source, reaction, viscous = (shrink(residual), shrink(reaction), shrink(viscous))
    stacked = jnp.concatenate([source, reaction[None], viscous[None]], 0)
    row_count, col_count = (source.shape[1], source.shape[2])
    for bit_index in range(lax.axis_size("gx").bit_length() - 1):
        stacked = pair_rows(stacked, bit_index)
    for bit_index in range(lax.axis_size("gy").bit_length() - 1):
        stacked = pair_cols(stacked, bit_index)
    whole_correction = level_solve(LOCAL, stacked[:2], stacked[2], stacked[3])
    correction = lax.dynamic_slice(
        whole_correction,
        (jnp.int32(0), lax.axis_index("gx") * row_count, lax.axis_index("gy") * col_count),
        (2, row_count, col_count),
    )
    for source, iterate, conduct, reaction, spacing, diagonal in reversed(stored):
        iterate = iterate + widen(correction)
        correction = (
            iterate + OMEGA * (source - operate(iterate, conduct, reaction, spacing)) / diagonal
        )
    return correction


def solution(mesh):
    placed = (P(None, "gx", "gy"), P("gx", "gy"), P("gx", "gy"), P("gx", "gy"))
    return jax.shard_map(
        per_device, mesh=mesh, in_specs=placed, out_specs=P(None, "gx", "gy"), check_vma=False
    )
```

profile of v0, /device:TPU:1, one launch (start us, length us, event | category | flops | bytes accessed | tf_op | source)
XLA Modules:
  0.0 397.2 jit_solution(17207723843118035474)
XLA Ops:
  1.5 5.4 %collective-permute-start = (f32[1,1,128]{2,1,0:T(1,128)S(1)}, f32[1,1,128]{2,1,0:T(1,128)S(1)}, u32[]{:S(2)}, u32[]{:S(2)}) collective-permute-start(f32[1,1,128]{2,1,0:T(1,128)S(1)} %get-tuple-element.81), channel_id=1, source_target_pairs={{0,32},{32,64},{64,96},{96,128},{128,160},{160,192},{192,224},{224... | collective-permute-start | bytes 1544 | tf_op jit(solution)/shard_map/ppermute | solution.py:22
  6.9 4.7 %collective-permute-start.1 = (f32[1,1,128]{2,1,0:T(1,128)S(1)}, f32[1,1,128]{2,1,0:T(1,128)S(1)}, u32[]{:S(2)}, u32[]{:S(2)}) collective-permute-start(f32[1,1,128]{2,1,0:T(1,128)S(1)} %get-tuple-element.82), channel_id=1, source_target_pairs={{32,0},{64,32},{96,64},{128,96},{160,128},{192,160},{224,192},{256... | collective-permute-start | bytes 1544 | tf_op jit(solution)/shard_map/ppermute | solution.py:23
  12.4 5.6 %reshape.396 = f32[64,2,64,2]{3,2,1,0:T(8,128)} reshape(f32[128,128]{1,0:T(8,128)S(1)} %broadcast_multiply_fusion) | data formatting | bytes 131072 | tf_op jit(solution)/shard_map/reshape | solution.py:69
  29.0 5.6 %reshape.395 = f32[64,2,64,2]{3,2,1,0:T(8,128)} reshape(f32[128,128]{1,0:T(8,128)S(1)} %copy-done) | data formatting | bytes 131072 | tf_op jit(solution)/shard_map/reshape | solution.py:69
  58.9 4.8 %collective-permute-start.10 = (f32[1,66,1]{2,1,0:T(8,128)S(1)}, f32[1,66,1]{2,1,0:T(8,128)S(1)}, u32[]{:S(2)}, u32[]{:S(2)}) collective-permute-start(f32[1,66,1]{2,1,0:T(8,128)S(1)} %get-tuple-element.87), channel_id=1, source_target_pairs={{0,1},{1,2},{2,3},{3,4},{4,5},{5,6},{6,7},{7,8},{8,9},{9,10},{10,1... | collective-permute-start | bytes 800 | tf_op jit(solution)/shard_map/ppermute | solution.py:22
  72.8 5.4 %collective-permute-done.5 = f32[2,1,128]{1,2,0:T(8,128)S(1)} collective-permute-done((f32[2,1,128]{1,2,0:T(8,128)S(1)}, f32[2,1,128]{1,2,0:T(8,128)S(1)}, u32[]{:S(2)}, u32[]{:S(2)}) %collective-permute-start.5) | collective-permute-done | bytes 1056 | tf_op jit(solution)/shard_map/ppermute | solution.py:23
  87.5 9.8 %reshape.394 = f32[2,64,2,64,2]{4,3,2,1,0:T(8,128)} reshape(f32[2,128,128]{2,1,0:T(8,128)S(1)} %copy.163) | data formatting | bytes 262144 | tf_op jit(solution)/shard_map/reshape | solution.py:69
  97.3 4.6 %reduce_sum.360 = f32[2,64,64]{2,1,0:T(8,128)S(1)} reduce(f32[2,64,2,64,2]{4,3,2,1,0:T(8,128)} %reshape.394, f32[]{:T(128)} %constant.201.clone.1), dimensions={2,4}, to_apply=%region_0.0 | reduce | flops 24576 | bytes 163844 | tf_op jit(solution)/shard_map/reduce_sum | solution.py:70
  131.3 4.8 %collective-permute-start.22 = (f32[2,34,1]{2,1,0:T(8,128)S(1)}, f32[2,34,1]{2,1,0:T(8,128)S(1)}, u32[]{:S(2)}, u32[]{:S(2)}) collective-permute-start(f32[2,34,1]{2,1,0:T(8,128)S(1)} %get-tuple-element.85), channel_id=1, source_target_pairs={{0,1},{1,2},{2,3},{3,4},{4,5},{5,6},{6,7},{7,8},{8,9},{9,10},{10,1... | collective-permute-start | bytes 824 | tf_op jit(solution)/shard_map/ppermute | solution.py:22
  151.5 4.6 %collective-permute-start.30 = (f32[2,18,1]{2,1,0:T(8,128)S(1)}, f32[2,18,1]{2,1,0:T(8,128)S(1)}, u32[]{:S(2)}, u32[]{:S(2)}) collective-permute-start(f32[2,18,1]{2,1,0:T(8,128)S(1)} %get-tuple-element.109), channel_id=1, source_target_pairs={{0,1},{1,2},{2,3},{3,4},{4,5},{5,6},{6,7},{7,8},{8,9},{9,10},{10,1... | collective-permute-start | bytes 440 | tf_op jit(solution)/shard_map/ppermute | solution.py:22
  164.0 5.7 %collective-permute-start.33 = (f32[4,16,8]{2,1,0:T(8,128)S(1)}, f32[4,16,8]{2,1,0:T(8,128)S(1)}, u32[]{:S(2)}, u32[]{:S(2)}) collective-permute-start(f32[4,16,8]{2,1,0:T(8,128)S(1)} %pad_maximum_fusion.58), channel_id=1, source_target_pairs={{0,64},{64,0},{32,96},{96,32},{128,192},{192,128},{160,224},{224,1... | collective-permute-start | bytes 6152 | tf_op jit(solution)/shard_map/ppermute | solution.py:35
  171.6 9.0 %collective-permute-start.34 = (f32[4,32,8]{1,2,0:T(8,128)S(1)}, f32[4,32,8]{1,2,0:T(8,128)S(1)}, u32[]{:S(2)}, u32[]{:S(2)}) collective-permute-start(f32[4,32,8]{1,2,0:T(8,128)S(1)} %pad_maximum_fusion.80), channel_id=1, source_target_pairs={{0,128},{128,0},{32,160},{160,32},{64,192},{192,64},{96,224},{224,... | collective-permute-start | bytes 12296 | tf_op jit(solution)/shard_map/ppermute | solution.py:35
  181.8 5.8 %collective-permute-start.35 = (f32[4,64,8]{1,2,0:T(8,128)S(1)}, f32[4,64,8]{1,2,0:T(8,128)S(1)}, u32[]{:S(2)}, u32[]{:S(2)}) collective-permute-start(f32[4,64,8]{1,2,0:T(8,128)S(1)} %pad_maximum_fusion.81), channel_id=1, source_target_pairs={{0,256},{256,0},{32,288},{288,32},{64,320},{320,64},{96,352},{352,... | collective-permute-start | bytes 24584 | tf_op jit(solution)/shard_map/ppermute | solution.py:35
  201.0 7.9 %collective-permute-start.38 = (f32[4,128,32]{1,2,0:T(8,128)S(1)}, f32[4,128,32]{1,2,0:T(8,128)S(1)}, u32[]{:S(2)}, u32[]{:S(2)}) collective-permute-start(f32[4,128,32]{1,2,0:T(8,128)S(1)} %pad_maximum_fusion.38), channel_id=1, source_target_pairs={{0,4},{4,0},{1,5},{5,1},{2,6},{6,2},{3,7},{7,3},{8,12},{12,8},{9,1... | collective-permute-start | bytes 196616 | tf_op jit(solution)/shard_map/ppermute | solution.py:35
  210.7 5.2 %collective-permute-start.39 = (f32[4,128,64]{1,2,0:T(8,128)S(1)}, f32[4,128,64]{1,2,0:T(8,128)S(1)}, u32[]{:S(2)}, u32[]{:S(2)}) collective-permute-start(f32[4,128,64]{1,2,0:T(8,128)S(1)} %pad_maximum_fusion.18), channel_id=1, source_target_pairs={{0,8},{8,0},{1,9},{9,1},{2,10},{10,2},{3,11},{11,3},{4,12},{12,4},... | collective-permute-start | bytes 393224 | tf_op jit(solution)/shard_map/ppermute | solution.py:35
  218.3 5.0 %collective-permute-start.40 = (f32[4,128,128]{1,2,0:T(8,128)S(1)}, f32[4,128,128]{1,2,0:T(8,128)S(1)}, u32[]{:S(2)}, u32[]{:S(2)}) collective-permute-start(f32[4,128,128]{1,2,0:T(8,128)S(1)} %pad_maximum_fusion), channel_id=1, source_target_pairs={{0,16},{16,0},{1,17},{17,1},{2,18},{18,2},{3,19},{19,3},{4,20},{20... | collective-permute-start | bytes 786440 | tf_op jit(solution)/shard_map/ppermute | solution.py:35
  230.6 9.8 %reshape_squeeze.6 = f32[64,2,128,2]{3,2,1,0:T(8,128)} reshape(f32[1,128,256]{2,1,0:T(8,128)S(1)} %copy.167) | data formatting | bytes 262144 | tf_op jit(solution)/shard_map/reshape;squeeze | solution.py:69
  240.4 5.2 %reduce_sum.385 = f32[64,128]{1,0:T(8,128)} reduce(f32[64,2,128,2]{3,2,1,0:T(8,128)} %reshape_squeeze.6, f32[]{:T(128)} %constant.201.clone.1), dimensions={1,3}, to_apply=%region_13.0 | reduce | flops 24576 | bytes 163844 | tf_op jit(solution)/shard_map/reduce_sum | solution.py:70
  245.6 9.8 %reshape_squeeze.7 = f32[64,2,128,2]{3,2,1,0:T(8,128)} reshape(f32[1,128,256]{2,1,0:T(8,128)S(1)} %copy.168) | data formatting | bytes 262144 | tf_op jit(solution)/shard_map/reshape;squeeze | solution.py:69
  274.1 18.9 %reshape.400 = f32[2,64,2,128,2]{4,3,2,1,0:T(8,128)} reshape(f32[2,128,256]{2,1,0:T(8,128)} %copy.166) | data formatting | bytes 524288 | tf_op jit(solution)/shard_map/reshape | solution.py:69
  292.9 8.0 %reduce_sum.384 = f32[2,64,128]{2,1,0:T(8,128)S(1)} reduce(f32[2,64,2,128,2]{4,3,2,1,0:T(8,128)} %reshape.400, f32[]{:T(128)} %constant.201.clone.1), dimensions={2,4}, to_apply=%region_12.0 | reduce | flops 49152 | bytes 327684 | tf_op jit(solution)/shard_map/reduce_sum | solution.py:70
  301.2 5.6 %reshape.401 = f32[2,32,2,64,2]{4,3,2,1,0:T(8,128)} reshape(f32[2,64,128]{2,1,0:T(8,128)S(1)} %fusion.68) | data formatting | bytes 131072 | tf_op jit(solution)/shard_map/reshape | solution.py:69
  317.2 12.3 %collective-permute-start.41 = (f32[2,1,16]{2,1,0:T(1,128)S(1)}, f32[2,1,16]{2,1,0:T(1,128)S(1)}, u32[]{:S(2)}, u32[]{:S(2)}) collective-permute-start(f32[2,1,16]{2,1,0:T(1,128)S(1)} %get-tuple-element.113), channel_id=1, source_target_pairs={{0,32},{32,64},{64,96},{96,128},{128,160},{160,192},{192,224},{224... | collective-permute-start | bytes 392 | tf_op jit(solution)/shard_map/ppermute | solution.py:22
  367.3 4.8 %collective-permute-start.51 = (f32[2,66,1]{2,1,0:T(8,128)S(1)}, f32[2,66,1]{2,1,0:T(8,128)S(1)}, u32[]{:S(2)}, u32[]{:S(2)}) collective-permute-start(f32[2,66,1]{2,1,0:T(8,128)S(1)} %get-tuple-element.67), channel_id=1, source_target_pairs={{0,1},{1,2},{2,3},{3,4},{4,5},{5,6},{6,7},{7,8},{8,9},{9,10},{10,1... | collective-permute-start | bytes 1592 | tf_op jit(solution)/shard_map/ppermute | solution.py:22
  (419 shorter events, 225.9 us)
Async XLA Ops:
  1.5 52.6 %collective-permute-start = (f32[1,1,128]{2,1,0:T(1,128)S(1)}, f32[1,1,128]{2,1,0:T(1,128)S(1)}, u32[]{:S(2)}, u32[]{:S(2)}) collective-permute-start(f32[1,1,128]{2,1,0:T(1,128)S(1)} %get-tuple-element.81), channel_id=1, source_target_pairs={{0,32},{32,64},{64,96},{96,128},{128,160},{160,192},{192,224},{224... | collective-permute-start | bytes 1544 | tf_op jit(solution)/shard_map/ppermute | solution.py:22
  6.9 47.2 %collective-permute-start.1 = (f32[1,1,128]{2,1,0:T(1,128)S(1)}, f32[1,1,128]{2,1,0:T(1,128)S(1)}, u32[]{:S(2)}, u32[]{:S(2)}) collective-permute-start(f32[1,1,128]{2,1,0:T(1,128)S(1)} %get-tuple-element.82), channel_id=1, source_target_pairs={{32,0},{64,32},{96,64},{128,96},{160,128},{192,160},{224,192},{256... | collective-permute-start | bytes 1544 | tf_op jit(solution)/shard_map/ppermute | solution.py:23
  20.9 27.9 %collective-permute-start.8 = (f32[1,1,64]{2,1,0:T(1,128)S(1)}, f32[1,1,64]{2,1,0:T(1,128)S(1)}, u32[]{:S(2)}, u32[]{:S(2)}) collective-permute-start(f32[1,1,64]{2,1,0:T(1,128)S(1)} %get-tuple-element.105), channel_id=1, source_target_pairs={{0,32},{32,64},{64,96},{96,128},{128,160},{160,192},{192,224},{224... | collective-permute-start | bytes 776 | tf_op jit(solution)/shard_map/ppermute | solution.py:22
  24.5 13.1 %collective-permute-start.24 = (f32[1,1,16]{2,1,0:T(1,128)S(1)}, f32[1,1,16]{2,1,0:T(1,128)S(1)}, u32[]{:S(2)}, u32[]{:S(2)}) collective-permute-start(f32[1,1,16]{2,1,0:T(1,128)S(1)} %get-tuple-element.129), channel_id=1, source_target_pairs={{0,32},{32,64},{64,96},{96,128},{128,160},{160,192},{192,224},{224... | collective-permute-start | bytes 200 | tf_op jit(solution)/shard_map/ppermute | solution.py:22
  26.5 14.4 %collective-permute-start.25 = (f32[1,1,16]{2,1,0:T(1,128)S(1)}, f32[1,1,16]{2,1,0:T(1,128)S(1)}, u32[]{:S(2)}, u32[]{:S(2)}) collective-permute-start(f32[1,1,16]{2,1,0:T(1,128)S(1)} %get-tuple-element.130), channel_id=1, source_target_pairs={{32,0},{64,32},{96,64},{128,96},{160,128},{192,160},{224,192},{256... | collective-permute-start | bytes 200 | tf_op jit(solution)/shard_map/ppermute | solution.py:23
  42.9 7.2 %collective-permute-start.9 = (f32[1,1,64]{2,1,0:T(1,128)S(1)}, f32[1,1,64]{2,1,0:T(1,128)S(1)}, u32[]{:S(2)}, u32[]{:S(2)}) collective-permute-start(f32[1,1,64]{2,1,0:T(1,128)S(1)} %get-tuple-element.106), channel_id=1, source_target_pairs={{32,0},{64,32},{96,64},{128,96},{160,128},{192,160},{224,192},{256... | collective-permute-start | bytes 776 | tf_op jit(solution)/shard_map/ppermute | solution.py:23
  45.8 82.5 %collective-permute-start.26 = (f32[1,18,1]{2,1,0:T(8,128)S(1)}, f32[1,18,1]{2,1,0:T(8,128)S(1)}, u32[]{:S(2)}, u32[]{:S(2)}) collective-permute-start(f32[1,18,1]{2,1,0:T(8,128)S(1)} %get-tuple-element.123), channel_id=1, source_target_pairs={{0,1},{1,2},{2,3},{3,4},{4,5},{5,6},{6,7},{7,8},{8,9},{9,10},{10,1... | collective-permute-start | bytes 224 | tf_op jit(solution)/shard_map/ppermute | solution.py:22
  48.8 79.5 %collective-permute-start.27 = (f32[1,18,1]{2,1,0:T(8,128)S(1)}, f32[1,18,1]{2,1,0:T(8,128)S(1)}, u32[]{:S(2)}, u32[]{:S(2)}) collective-permute-start(f32[1,18,1]{2,1,0:T(8,128)S(1)} %get-tuple-element.124), channel_id=1, source_target_pairs={{1,0},{2,1},{3,2},{4,3},{5,4},{6,5},{7,6},{8,7},{9,8},{10,9},{11,1... | collective-permute-start | bytes 224 | tf_op jit(solution)/shard_map/ppermute | solution.py:23
  50.1 55.1 %collective-permute-start.18 = (f32[1,34,1]{2,1,0:T(8,128)S(1)}, f32[1,34,1]{2,1,0:T(8,128)S(1)}, u32[]{:S(2)}, u32[]{:S(2)}) collective-permute-start(f32[1,34,1]{2,1,0:T(8,128)S(1)} %get-tuple-element.111), channel_id=1, source_target_pairs={{0,1},{1,2},{2,3},{3,4},{4,5},{5,6},{6,7},{7,8},{8,9},{9,10},{10,1... | collective-permute-start | bytes 416 | tf_op jit(solution)/shard_map/ppermute | solution.py:22
  58.9 6.6 %collective-permute-start.10 = (f32[1,66,1]{2,1,0:T(8,128)S(1)}, f32[1,66,1]{2,1,0:T(8,128)S(1)}, u32[]{:S(2)}, u32[]{:S(2)}) collective-permute-start(f32[1,66,1]{2,1,0:T(8,128)S(1)} %get-tuple-element.87), channel_id=1, source_target_pairs={{0,1},{1,2},{2,3},{3,4},{4,5},{5,6},{6,7},{7,8},{8,9},{9,10},{10,1... | collective-permute-start | bytes 800 | tf_op jit(solution)/shard_map/ppermute | solution.py:22
  63.7 6.5 %collective-permute-start.11 = (f32[1,66,1]{2,1,0:T(8,128)S(1)}, f32[1,66,1]{2,1,0:T(8,128)S(1)}, u32[]{:S(2)}, u32[]{:S(2)}) collective-permute-start(f32[1,66,1]{2,1,0:T(8,128)S(1)} %get-tuple-element.88), channel_id=1, source_target_pairs={{1,0},{2,1},{3,2},{4,3},{5,4},{6,5},{7,6},{8,7},{9,8},{10,9},{11,1... | collective-permute-start | bytes 800 | tf_op jit(solution)/shard_map/ppermute | solution.py:23
  65.5 7.2 %collective-permute-start.4 = (f32[2,1,128]{1,2,0:T(8,128)S(1)}, f32[2,1,128]{1,2,0:T(8,128)S(1)}, u32[]{:S(2)}, u32[]{:S(2)}) collective-permute-start(f32[2,1,128]{1,2,0:T(8,128)S(1)} %get-tuple-element.65), channel_id=1, source_target_pairs={{0,32},{32,64},{64,96},{96,128},{128,160},{160,192},{192,224},{224... | collective-permute-start | bytes 3080 | tf_op jit(solution)/shard_map/ppermute | solution.py:22
  70.2 8.0 %collective-permute-start.5 = (f32[2,1,128]{1,2,0:T(8,128)S(1)}, f32[2,1,128]{1,2,0:T(8,128)S(1)}, u32[]{:S(2)}, u32[]{:S(2)}) collective-permute-start(f32[2,1,128]{1,2,0:T(8,128)S(1)} %get-tuple-element.66), channel_id=1, source_target_pairs={{32,0},{64,32},{96,64},{128,96},{160,128},{192,160},{224,192},{256... | collective-permute-start | bytes 3080 | tf_op jit(solution)/shard_map/ppermute | solution.py:23
  84.1 23.1 %collective-permute-start.19 = (f32[1,34,1]{2,1,0:T(8,128)S(1)}, f32[1,34,1]{2,1,0:T(8,128)S(1)}, u32[]{:S(2)}, u32[]{:S(2)}) collective-permute-start(f32[1,34,1]{2,1,0:T(8,128)S(1)} %get-tuple-element.112), channel_id=1, source_target_pairs={{1,0},{2,1},{3,2},{4,3},{5,4},{6,5},{7,6},{8,7},{9,8},{10,9},{11,1... | collective-permute-start | bytes 416 | tf_op jit(solution)/shard_map/ppermute | solution.py:23
  101.9 6.6 %collective-permute-start.12 = (f32[2,1,64]{2,1,0:T(1,128)S(1)}, f32[2,1,64]{2,1,0:T(1,128)S(1)}, u32[]{:S(2)}, u32[]{:S(2)}) collective-permute-start(f32[2,1,64]{2,1,0:T(1,128)S(1)} %get-tuple-element.79), channel_id=1, source_target_pairs={{0,32},{32,64},{64,96},{96,128},{128,160},{160,192},{192,224},{224... | collective-permute-start | bytes 1544 | tf_op jit(solution)/shard_map/ppermute | solution.py:22
  131.3 6.3 %collective-permute-start.22 = (f32[2,34,1]{2,1,0:T(8,128)S(1)}, f32[2,34,1]{2,1,0:T(8,128)S(1)}, u32[]{:S(2)}, u32[]{:S(2)}) collective-permute-start(f32[2,34,1]{2,1,0:T(8,128)S(1)} %get-tuple-element.85), channel_id=1, source_target_pairs={{0,1},{1,2},{2,3},{3,4},{4,5},{5,6},{6,7},{7,8},{8,9},{9,10},{10,1... | collective-permute-start | bytes 824 | tf_op jit(solution)/shard_map/ppermute | solution.py:22
  141.7 6.4 %collective-permute-start.28 = (f32[2,1,16]{2,1,0:T(1,128)S(1)}, f32[2,1,16]{2,1,0:T(1,128)S(1)}, u32[]{:S(2)}, u32[]{:S(2)}) collective-permute-start(f32[2,1,16]{2,1,0:T(1,128)S(1)} %get-tuple-element.116), channel_id=1, source_target_pairs={{0,32},{32,64},{64,96},{96,128},{128,160},{160,192},{192,224},{224... | collective-permute-start | bytes 392 | tf_op jit(solution)/shard_map/ppermute | solution.py:22
  164.0 7.3 %collective-permute-start.33 = (f32[4,16,8]{2,1,0:T(8,128)S(1)}, f32[4,16,8]{2,1,0:T(8,128)S(1)}, u32[]{:S(2)}, u32[]{:S(2)}) collective-permute-start(f32[4,16,8]{2,1,0:T(8,128)S(1)} %pad_maximum_fusion.58), channel_id=1, source_target_pairs={{0,64},{64,0},{32,96},{96,32},{128,192},{192,128},{160,224},{224,1... | collective-permute-start | bytes 6152 | tf_op jit(solution)/shard_map/ppermute | solution.py:35
  171.6 10.1 %collective-permute-start.34 = (f32[4,32,8]{1,2,0:T(8,128)S(1)}, f32[4,32,8]{1,2,0:T(8,128)S(1)}, u32[]{:S(2)}, u32[]{:S(2)}) collective-permute-start(f32[4,32,8]{1,2,0:T(8,128)S(1)} %pad_maximum_fusion.80), channel_id=1, source_target_pairs={{0,128},{128,0},{32,160},{160,32},{64,192},{192,64},{96,224},{224,... | collective-permute-start | bytes 12296 | tf_op jit(solution)/shard_map/ppermute | solution.py:35
  181.8 8.4 %collective-permute-start.35 = (f32[4,64,8]{1,2,0:T(8,128)S(1)}, f32[4,64,8]{1,2,0:T(8,128)S(1)}, u32[]{:S(2)}, u32[]{:S(2)}) collective-permute-start(f32[4,64,8]{1,2,0:T(8,128)S(1)} %pad_maximum_fusion.81), channel_id=1, source_target_pairs={{0,256},{256,0},{32,288},{288,32},{64,320},{320,64},{96,352},{352,... | collective-permute-start | bytes 24584 | tf_op jit(solution)/shard_map/ppermute | solution.py:35
  201.0 9.6 %collective-permute-start.38 = (f32[4,128,32]{1,2,0:T(8,128)S(1)}, f32[4,128,32]{1,2,0:T(8,128)S(1)}, u32[]{:S(2)}, u32[]{:S(2)}) collective-permute-start(f32[4,128,32]{1,2,0:T(8,128)S(1)} %pad_maximum_fusion.38), channel_id=1, source_target_pairs={{0,4},{4,0},{1,5},{5,1},{2,6},{6,2},{3,7},{7,3},{8,12},{12,8},{9,1... | collective-permute-start | bytes 196616 | tf_op jit(solution)/shard_map/ppermute | solution.py:35
  210.7 7.5 %collective-permute-start.39 = (f32[4,128,64]{1,2,0:T(8,128)S(1)}, f32[4,128,64]{1,2,0:T(8,128)S(1)}, u32[]{:S(2)}, u32[]{:S(2)}) collective-permute-start(f32[4,128,64]{1,2,0:T(8,128)S(1)} %pad_maximum_fusion.18), channel_id=1, source_target_pairs={{0,8},{8,0},{1,9},{9,1},{2,10},{10,2},{3,11},{11,3},{4,12},{12,4},... | collective-permute-start | bytes 393224 | tf_op jit(solution)/shard_map/ppermute | solution.py:35
  218.3 9.4 %collective-permute-start.40 = (f32[4,128,128]{1,2,0:T(8,128)S(1)}, f32[4,128,128]{1,2,0:T(8,128)S(1)}, u32[]{:S(2)}, u32[]{:S(2)}) collective-permute-start(f32[4,128,128]{1,2,0:T(8,128)S(1)} %pad_maximum_fusion), channel_id=1, source_target_pairs={{0,16},{16,0},{1,17},{17,1},{2,18},{18,2},{3,19},{19,3},{4,20},{20... | collective-permute-start | bytes 786440 | tf_op jit(solution)/shard_map/ppermute | solution.py:35
  317.2 14.2 %collective-permute-start.41 = (f32[2,1,16]{2,1,0:T(1,128)S(1)}, f32[2,1,16]{2,1,0:T(1,128)S(1)}, u32[]{:S(2)}, u32[]{:S(2)}) collective-permute-start(f32[2,1,16]{2,1,0:T(1,128)S(1)} %get-tuple-element.113), channel_id=1, source_target_pairs={{0,32},{32,64},{64,96},{96,128},{128,160},{160,192},{192,224},{224... | collective-permute-start | bytes 392 | tf_op jit(solution)/shard_map/ppermute | solution.py:22
  (90 other events, 2177.5 us)
where the time goes:
time: 404 us; the launch traced here: 397 us
  starting transfers between devices  186 us (46%)
  local copies, waits for them, and re-layouts  84.2 us (21%)
  waiting for transfers between devices  72.4 us (18%)
  other arithmetic  51 us (13%)
    ppermute x24, starting transfers between devices, extended(): before = lax.ppermute(last, axis, up)  95.2 us
    ppermute x24, waiting for transfers between devices, extended(): after = lax.ppermute(leading, axis, down)  55.2 us
    reshape x10, local copies, waits for them, and re-layouts, shrink(): blocks = field.reshape(field.shape[:-2] + (size_x // 2, 2, size_y // 2, 2))  49.2 us
    ppermute x9, starting transfers between devices, swapped(): return lax.ppermute(block, axis, route)  48.7 us
    ppermute x24, starting transfers between devices, extended(): after = lax.ppermute(leading, axis, down)  42.5 us
    reduce_sum x24, other arithmetic, shrink(): return jnp.mean(blocks, axis=(-3, -1))  35.5 us
    another operation x2, local copies, waits for them, and re-layouts, shrink(): blocks = field.reshape(field.shape[:-2] + (size_x // 2, 2, size_y // 2, 2))  19.6 us
    ppermute x9, waiting for transfers between devices, swapped(): return lax.ppermute(block, axis, route)  17 us
  transfers between devices with their start and end apart: 57, of which 29 were waited for; matrix products, arithmetic and copies ran while one was open for 10% of the time, Pallas kernels for 0%

commit v1 on v0

v1 whole, which is shorter than its diff:
```python
import functools

import jax
import jax.numpy as jnp
from jax import lax
from jax.experimental import pallas as pl
from jax.experimental.pallas import tpu as pltpu
from jax.sharding import PartitionSpec as P

TILE = 128
OMEGA = 0.8
KEEP = 1.0 - OMEGA
HALO = 16
ROWS = TILE + 2 * HALO
F32 = jnp.float32
MESH = pl.DeviceIdType.MESH
DIRECTIONS = ((-1, 0), (1, 0), (0, -1), (0, 1), (-1, -1), (-1, 1), (1, -1), (1, 1))
SOURCE_OF = {step: i for i, step in enumerate(DIRECTIONS)}


def iota(shape, dim):
    return lax.broadcasted_iota(jnp.int32, shape, dim)


def roll_rows(x, k):
    return pltpu.roll(x, k % x.shape[0], axis=0)


def roll_lanes(x, k):
    return pltpu.roll(x, k % x.shape[1], axis=1)


def exact_dot(a, b, transposed=False):
    dims = (((1,), (1,)), ((), ())) if transposed else (((1,), (0,)), ((), ()))
    return lax.dot_general(
        a, b, dims, precision=lax.Precision.HIGHEST, preferred_element_type=F32
    )


def coefficients(viscous, reaction, level, pitch, closed=None):
    spacing = 0.25**level
    up = jnp.minimum(viscous, roll_rows(viscous, 1)) * spacing
    left = jnp.minimum(viscous, roll_lanes(viscous, pitch)) * spacing
    if closed is not None:
        up = jnp.where(closed[0], 0.0, up)
        left = jnp.where(closed[1], 0.0, left)
    down = roll_rows(up, -1)
    right = roll_lanes(left, -pitch)
    weight = OMEGA / (reaction + ((up + down) + (left + right)))
    return up, down, left, right, weight


def inflow(iterate, faces, pitch):
    up, down, left, right = faces[:4]
    return (up * roll_rows(iterate, 1) + down * roll_rows(iterate, -1)) + (
        left * roll_lanes(iterate, pitch) + right * roll_lanes(iterate, -pitch)
    )


def residual_of(source, iterate, faces, pitch):
    return KEEP * source + inflow(iterate, faces, pitch)


def swept(source, iterate, faces, pitch):
    return KEEP * iterate + faces[4] * (source + inflow(iterate, faces, pitch))


def kernel(
    gx_count,
    gy_count,
    rhs_hbm,
    shift_hbm,
    visc_hbm,
    wet_ref,
    out_ref,
    own,
    strips,
    coef_block,
    row_halo,
    col_halo,
    corner_halo,
    coef_halo,
    block,
    block_halo,
    gx_coef,
    gx_source,
    gy_coef,
    gy_source,
    ext,
    pooled,
    level0,
    level1,
    level2,
    padded,
    spread,
    coarse,
    load_sem,
    send1,
    recv1,
    send2,
    recv2,
    send3,
    recv3,
    gather_send,
    gather_recv,
):
    a = lax.axis_index("gx")
    b = lax.axis_index("gy")

    def at(da, db):
        return (lax.rem(a + da + gx_count, gx_count), lax.rem(b + db + gy_count, gy_count))

    barrier = pltpu.get_barrier_semaphore()

    def greet_gx(k, carry):
        peer = (lax.rem(a + k, gx_count), b)
        pl.semaphore_signal(barrier, inc=1, device_id=peer, device_id_type=MESH)
        return carry

    def greet_gy(k, carry):
        peer = (a, lax.rem(b + k, gy_count))
        pl.semaphore_signal(barrier, inc=1, device_id=peer, device_id_type=MESH)
        return carry

    for da, db in DIRECTIONS[4:]:
        pl.semaphore_signal(barrier, inc=1, device_id=at(da, db), device_id_type=MESH)
    lax.fori_loop(1, gx_count, greet_gx, 0)
    lax.fori_loop(1, gy_count, greet_gy, 0)

    loads = [
        pltpu.make_async_copy(rhs_hbm, own.at[pl.ds(0, 2)], load_sem.at[0]),
        pltpu.make_async_copy(shift_hbm, own.at[2], load_sem.at[1]),
        pltpu.make_async_copy(visc_hbm, own.at[3], load_sem.at[2]),
    ]
    for load in loads:
        load.start()

    padded[...] = jnp.zeros_like(padded)
    for load in loads:
        load.wait()

    wet = wet_ref[0, 0].astype(F32)
    for f in (0, 1, 3):
        own[f] = own[f] * wet

    slot = iota((64, 128), 1) // HALO
    for side, first in ((0, 0), (1, TILE - HALO)):
        packed = jnp.zeros((64, 128), F32)
        for half in range(2):
            for f in range(4):
                place = half * 64 + f * HALO
                moved = roll_lanes(own[f, half * 64 : half * 64 + 64, :], place - first)
                packed = jnp.where(slot == half * 4 + f, moved, packed)
        strips[side] = packed

    lane_to_col = jnp.where(iota((16, 128), 1) // 8 == iota((16, 128), 0), 0.125, 0.0)
    target = iota((128, 128), 1)
    target_row = jnp.where(target < 48, target, jnp.where(target < 96, target - 48, -1)) - 16
    row_to_lane = jnp.where(iota((128, 128), 0) // 8 == target_row, 0.125, 0.0)
    for i, f in enumerate((2, 3)):
        coef_block[i] = exact_dot(exact_dot(lane_to_col, own[f], True), row_to_lane)

    pl.semaphore_wait(barrier, 4 + gx_count - 1 + gy_count - 1)

    copies1 = []

    def send(src, dst, sends, recvs, i, da, db):
        copy = pltpu.make_async_remote_copy(
            src_ref=src,
            dst_ref=dst,
            send_sem=sends.at[i],
            recv_sem=recvs.at[i],
            device_id=at(da, db),
            device_id_type=MESH,
        )
        copy.start()
        return copy

    for i, (da, db) in enumerate(DIRECTIONS):
        if db == 0:
            first = 0 if da < 0 else TILE - HALO
            src, dst = own.at[:, pl.ds(first, HALO)], row_halo.at[i]
        elif da == 0:
            src, dst = strips.at[0 if db < 0 else 1], col_halo.at[i - 2]
        else:
            first = 0 if da < 0 else 64 - HALO
            src = strips.at[0 if db < 0 else 1, pl.ds(first, HALO)]
            dst = corner_halo.at[i - 4]
        copies1.append(send(src, dst, send1, recv1, i, da, db))
    copies2 = [
        send(coef_block, coef_halo.at[i], send2, recv2, i, da, db)
        for i, (da, db) in enumerate(DIRECTIONS)
    ]

    lane = iota((1, 128), 1)
    inside_up = (a > 0).astype(F32)
    inside_down = (a < gx_count - 1).astype(F32)
    inside_left = (b > 0).astype(F32)
    inside_right = (b < gy_count - 1).astype(F32)
    for f in range(4):
        ext[f, HALO : HALO + TILE, 0:128] = own[f]

    for copy in copies1:
        copy.wait()

    from_down, from_up = row_halo[0], row_halo[1]
    visible = (lane < HALO).astype(F32) * inside_right + (lane >= TILE - HALO).astype(
        F32
    ) * inside_left
    for f in range(4):
        top, bottom = from_up[f], from_down[f]
        if f == 3:
            top, bottom = top * inside_up, bottom * inside_down
        ext[f, 0:HALO, 0:128] = top
        ext[f, HALO + TILE :, 0:128] = bottom
        fill = 1.0 if f == 2 else 0.0

        def side(right, left, half):
            place = half * 64 + f * HALO
            r = roll_lanes(right, -place)
            l = roll_lanes(left, TILE - HALO - place)
            both = jnp.where(lane < HALO, r, jnp.where(lane >= TILE - HALO, l, fill))
            return both * visible if f == 3 else both

        for half in range(2):
            ext[f, HALO + half * 64 : HALO + half * 64 + 64, 128:256] = side(
                col_halo[0], col_halo[1], half
            )
        top = side(corner_halo[2], corner_halo[3], 1)
        bottom = side(corner_halo[0], corner_halo[1], 0)
        if f == 3:
            top, bottom = top * inside_up, bottom * inside_down
        ext[f, 0:HALO, 128:256] = top
        ext[f, HALO + TILE :, 128:256] = bottom

    def pool(x, i, pitch, start=0, rows=None):
        n = x.shape[0]
        width = x.shape[1]
        rows = n // 2 if rows is None else rows
        parts = []
        for t in range(width // 128):
            pooled[i, t, 0:n, :] = x[:, t * 128 : t * 128 + 128]
            parts.append(
                pooled[i, t, pl.ds(start, rows, stride=2), :]
                + pooled[i, t, pl.ds(start + 1, rows, stride=2), :]
            )
        y = parts[0] if len(parts) == 1 else jnp.concatenate(parts, axis=1)
        return y if pitch is None else (y + roll_lanes(y, -pitch)) * 0.25

    fields = [ext[f] for f in range(4)]
    stores = (level0, level1, level2)
    for level in range(3):
        pitch = 2**level
        keep = stores[level]
        faces = coefficients(fields[3], fields[2], level, pitch)
        for j in range(5):
            keep[j] = faces[j]
        residuals = []
        for c in range(2):
            iterate = fields[c] * faces[4]
            keep[5 + c] = fields[c]
            residuals.append(residual_of(fields[c], iterate, faces, pitch))
        if level < 2:
            fields = [
                pool(x, i, pitch) for i, x in enumerate((*residuals, fields[2], fields[3]))
            ]

    first = HALO // 4
    for c in range(2):
        padded[c * 48 + 16 : c * 48 + 32, :] = pool(residuals[c][:, 0:128], c, None, first, 16)
    lanes16 = iota((16, 128), 1)
    pick = jnp.where(
        (lanes16 // 8 == iota((16, 128), 0)) & (lanes16 % 4 == 0), 0.25, 0.0
    )
    block[...] = exact_dot(pick, padded[...], True)
    copies3 = [
        send(block, block_halo.at[i], send3, recv3, i, da, db)
        for i, (da, db) in enumerate(DIRECTIONS)
    ]

    def assembled(mine, theirs, fill, masks):
        lanes = iota((16, 128), 1)
        parts = [jnp.full((8, 128), fill, F32)]
        for db in (-1, 0, 1):
            above = theirs(SOURCE_OF[(1, -db)])
            below = theirs(SOURCE_OF[(-1, -db)])
            here = mine if db == 0 else theirs(SOURCE_OF[(0, -db)])
            if masks:
                above, below = above * inside_up, below * inside_down
            part = here + roll_lanes(above, -16) + roll_lanes(below, 16)
            if masks and db != 0:
                part = part * (inside_left if db < 0 else inside_right)
            parts.append(jnp.where(lanes < 96, part, fill))
        parts.append(jnp.full((8, 128), fill, F32))
        return jnp.concatenate(parts, axis=0)

    for copy in copies2:
        copy.wait()
    reaction = assembled(coef_block[0], lambda i: coef_halo[i, 0], 1.0, False)
    viscous = assembled(coef_block[1], lambda i: coef_halo[i, 1], 0.0, True)
    mid_faces = []
    for level in range(3, 6):
        pitch = 2 ** (level - 3)
        mid_faces.append(coefficients(viscous, reaction, level, pitch))
        reaction, viscous = pool(reaction, 2, pitch), pool(viscous, 3, pitch)

    def level6_row(x):
        lanes = iota((8, 128), 1)
        total = jnp.zeros((8, 128), F32)
        for c in range(2):
            for r in range(2):
                here = c * 48 + 16 + 8 * r
                there = 2 * a + (c * 32 + r - here + 128)
                only = jnp.where(lanes == here, x, 0.0)
                total = total + pltpu.roll(only, lax.rem(there, 128), axis=1)
        return total[3:4] + roll_lanes(total[4:5], 64)

    def gather(slots, index, axis, sem):
        count = gx_count if axis == "gx" else gy_count

        def copy_to(k):
            peer = (lax.rem(a + k, count), b) if axis == "gx" else (a, lax.rem(b + k, count))
            return pltpu.make_async_remote_copy(
                src_ref=slots.at[index],
                dst_ref=slots.at[index],
                send_sem=gather_send.at[sem],
                recv_sem=gather_recv.at[sem],
                device_id=peer,
                device_id_type=MESH,
            )

        def start(k, carry):
            copy_to(k).start()
            return carry

        lax.fori_loop(1, count, start, 0)

    def gathered(slots, axis, sem):
        count = gx_count if axis == "gx" else gy_count
        every = pltpu.make_async_remote_copy(
            src_ref=slots.at[pl.ds(0, count - 1)],
            dst_ref=slots.at[pl.ds(0, count - 1)],
            send_sem=gather_send.at[sem],
            recv_sem=gather_recv.at[sem],
            device_id=at(1, 0),
            device_id_type=MESH,
        )
        every.wait()

    gx_coef[a, 0:1, :] = level6_row(reaction)
    gx_coef[a, 1:2, :] = level6_row(viscous)
    gather(gx_coef, a, "gx", 0)
    gathered(gx_coef, "gx", 0)
    gy_coef[b] = jnp.sum(gx_coef[...], axis=0)
    gather(gy_coef, b, "gy", 1)

    for copy in copies3:
        copy.wait()
    sources = []
    source = assembled(block[...], lambda i: block_halo[i], 0.0, False)
    for level in range(3, 6):
        pitch = 2 ** (level - 3)
        faces = mid_faces[level - 3]
        sources.append(source)
        source = pool(residual_of(source, source * faces[4], faces, pitch), 0, pitch)

    gx_source[a] = level6_row(source)
    gather(gx_source, a, "gx", 2)

    def spread_rows(x):
        n = x.shape[0]
        parts = []
        for t in range(x.shape[1] // 128):
            piece = x[:, t * 128 : t * 128 + 128]
            spread[t, pl.ds(0, n, stride=2), :] = piece
            spread[t, pl.ds(1, n, stride=2), :] = piece
            parts.append(spread[t, 0 : 2 * n, :])
        return parts[0] if len(parts) == 1 else jnp.concatenate(parts, axis=1)

    def widened(x, pitch):
        odd = (iota((1, x.shape[1]), 1) & pitch) != 0
        return spread_rows(jnp.where(odd, roll_lanes(x, pitch), x))

    cols6 = 64

    def whole(read, i):
        for j in range(gy_count):
            row = read(j)
            coarse[i, 2 * j : 2 * j + 1, :] = row
            coarse[i, 2 * j + 1 : 2 * j + 2, :] = roll_lanes(row, 64)
        return coarse[i]

    if gy_count * 2 < cols6:
        coarse[...] = jnp.zeros_like(coarse)

    def solved_coefficients():
        gathered(gy_coef, "gy", 1)
        reaction = whole(lambda j: gy_coef[j, 0:1, :], 0)
        viscous = whole(lambda j: gy_coef[j, 1:2, :], 1)
        if gx_count * 2 < 32 or gy_count * 2 < cols6:
            reaction = jnp.where(reaction == 0.0, 1.0, reaction)
        result = []
        for level in range(6, 9):
            pitch = 2 ** (level - 6)
            n = viscous.shape[0]
            closed = (iota((n, 128), 0) == 0, iota((n, 128), 1) % 32 < pitch)
            faces = coefficients(viscous, reaction, level, pitch, closed)
            down = jnp.where(iota((n, 128), 0) == n - 1, 0.0, faces[1])
            result.append((faces[0], down, *faces[2:]))
            if level < 8:
                reaction, viscous = pool(reaction, 2, pitch), pool(viscous, 3, pitch)
        return result

    gathered(gx_source, "gx", 2)
    gy_source[b] = jnp.sum(gx_source[...], axis=0)
    gather(gy_source, b, "gy", 3)
    coarse_faces = solved_coefficients()

    col6 = iota((16, 64), 1)
    take_cols = jnp.where(col6 == 2 * b - 3 + iota((16, 64), 0) // 2, 1.0, 0.0)
    to_lane = iota((128, 128), 1)
    second = to_lane >= 48
    local_lane = jnp.where(second, to_lane - 48, to_lane)
    from_lane = jnp.where(second, 32, 0) + 2 * a - 2 + local_lane // 8
    take_rows = jnp.where((iota((128, 128), 0) == from_lane) & (to_lane < 96), 1.0, 0.0)
    row2 = iota((80, 128), 0)
    comp2 = row2 // 40
    wanted = comp2 * 48 + 16 + (row2 - comp2 * 40 + 4) // 2 - 4
    rows_back = jnp.where(iota((80, 128), 1) == wanted, 1.0, 0.0)
    fine = iota((64, 256), 1)
    fine = jnp.where(fine < 192, fine, fine - 256) + 256
    cols_back = jnp.where(iota((64, 256), 0) == 24 + fine // 8 - 32, 1.0, 0.0)

    gathered(gy_source, "gy", 3)
    source = whole(lambda j: gy_source[j], 2)
    coarse_sources = []
    for level in range(6, 8):
        pitch = 2 ** (level - 6)
        faces = coarse_faces[level - 6]
        coarse_sources.append(source)
        source = pool(residual_of(source, source * faces[4], faces, pitch), 0, pitch)
    up, down, left, right, weight = coarse_faces[2]
    scaled = (weight * up, weight * down, weight * left, weight * right)
    start = weight * source
    solution_now = start
    for _ in range(7):
        solution_now = (KEEP * solution_now + start) + inflow(solution_now, scaled, 4)
    for level in (7, 6):
        pitch = 2 ** (level - 6)
        faces = coarse_faces[level - 6]
        source = coarse_sources[level - 6]
        iterate = source * faces[4] + widened(solution_now, pitch)
        solution_now = swept(source, iterate, faces, pitch)

    correction = exact_dot(exact_dot(take_cols, solution_now), take_rows)
    for level in (5, 4, 3):
        pitch = 2 ** (level - 3)
        faces = mid_faces[level - 3]
        source = sources[level - 3]
        if level < 5:
            correction = widened(correction, pitch)
        correction = swept(source, source * faces[4] + correction, faces, pitch)

    both = exact_dot(exact_dot(rows_back, correction, True), cols_back)
    fine_now = [both[0:40], both[40:80]]
    for level in (2, 1, 0):
        pitch = 2**level
        keep = stores[level]
        faces = [keep[j] for j in range(5)]
        for c in range(2):
            source = keep[5 + c]
            correction = fine_now[c] if level == 2 else widened(fine_now[c], pitch)
            result = swept(source, source * faces[4] + correction, faces, pitch)
            if level == 0:
                out_ref[c] = result[HALO : HALO + TILE, 0:128]
            else:
                fine_now[c] = result


def solution(mesh):
    gx_count, gy_count = mesh.shape["gx"], mesh.shape["gy"]

    def per_device(right_side, shift_coef, viscosity, wet_tiles):
        hbm = pl.BlockSpec(memory_space=pl.ANY)
        dma = pltpu.SemaphoreType.DMA
        return pl.pallas_call(
            functools.partial(kernel, gx_count, gy_count),
            out_shape=jax.ShapeDtypeStruct((2, TILE, TILE), F32),
            in_specs=[hbm, hbm, hbm, pl.BlockSpec(memory_space=pltpu.SMEM)],
            out_specs=pl.BlockSpec(memory_space=pltpu.VMEM),
            scratch_shapes=[
                pltpu.VMEM((4, TILE, TILE), F32),
                pltpu.VMEM((2, 64, 128), F32),
                pltpu.VMEM((2, 16, 128), F32),
                pltpu.VMEM((2, 4, HALO, 128), F32),
                pltpu.VMEM((2, 64, 128), F32),
                pltpu.VMEM((4, HALO, 128), F32),
                pltpu.VMEM((8, 2, 16, 128), F32),
                pltpu.VMEM((16, 128), F32),
                pltpu.VMEM((8, 16, 128), F32),
                pltpu.VMEM((gx_count, 2, 128), F32),
                pltpu.VMEM((gx_count, 1, 128), F32),
                pltpu.VMEM((gy_count, 2, 128), F32),
                pltpu.VMEM((gy_count, 1, 128), F32),
                pltpu.VMEM((4, ROWS, 256), F32),
                pltpu.VMEM((4, 2, ROWS, 128), F32),
                pltpu.VMEM((7, ROWS, 256), F32),
                pltpu.VMEM((7, ROWS // 2, 256), F32),
                pltpu.VMEM((7, ROWS // 4, 256), F32),
                pltpu.VMEM((128, 128), F32),
                pltpu.VMEM((2, ROWS, 128), F32),
                pltpu.VMEM((3, 64, 128), F32),
                dma((3,)),
                dma((8,)),
                dma((8,)),
                dma((8,)),
                dma((8,)),
                dma((8,)),
                dma((8,)),
                dma((4,)),
                dma((4,)),
            ],
            compiler_params=pltpu.CompilerParams(collective_id=0, has_side_effects=True),
            name="vcycle",
        )(right_side, shift_coef, viscosity, wet_tiles)

    placed = (P(None, "gx", "gy"), P("gx", "gy"), P("gx", "gy"), P("gx", "gy"))
    return jax.shard_map(
        per_device, mesh=mesh, in_specs=placed, out_specs=P(None, "gx", "gy"), check_vma=False
    )
```

time: 404 us -> 44.4 us (0.11); the launches traced: 397 us -> 44.3 us
  starting transfers between devices: 186 us -> 0 us
  local copies, waits for them, and re-layouts: 84.2 us -> 1.57 us
  waiting for transfers between devices: 72.4 us -> 0 us
  other arithmetic: 51 us -> 0 us
  Pallas kernels: 0 us -> 42 us
    ppermute x57 -> x0, starting transfers between devices: 186 us -> none  [the longest x24 95.2 us: extended(): before = lax.ppermute(last, axis, up)]
    ppermute x57 -> x0, waiting for transfers between devices: 72.4 us -> none  [the longest x24 55.2 us: extended(): after = lax.ppermute(leading, axis, down)]
    reshape x24 -> x0, local copies, waits for them, and re-layouts: 50.2 us -> none  [the longest x10 49.2 us: shrink(): blocks = field.reshape(field.shape[:-2] + (size_x // 2, 2, size_y // 2, 2))]
    pallas_call x0 -> x1, Pallas kernels: none -> 42 us  [per_device(): pl.pallas_call(functools.partial(kernel, gx_count, gy_count), out_shape=j...]
    reduce_sum x24 -> x0, other arithmetic: 35.5 us -> none  [shrink(): return jnp.mean(blocks, axis=(-3, -1))]
    another operation x2 -> x0, local copies, waits for them, and re-layouts: 19.6 us -> none  [shrink(): blocks = field.reshape(field.shape[:-2] + (size_x // 2, 2, size_y // 2, 2))]
    add x32 -> x0, other arithmetic: 9.18 us -> none  [the longest x3 3.67 us: level_solve(): diagonal = reaction + spacing * jnp.sum(conduct, axis=0)]
    div x12 -> x0, local copies, waits for them, and re-layouts: 8.03 us -> none  [shrink(): return jnp.mean(blocks, axis=(-3, -1))]
  transfers between devices with their start and end apart: 57 -> 0, of which waited for: 29 -> 0; matrix products, arithmetic and copies ran while one was open for 10% -> 0% of each run, Pallas kernels for 0% -> 0%
where the time goes in v1:
time: 44.4 us; the launch traced here: 44.3 us
  Pallas kernels  42 us (95%)
  local copies, waits for them, and re-layouts  1.57 us (4%)
  between operations  0.66 us (1%)
    pallas_call x1, Pallas kernels, per_device(): pl.pallas_call(functools.partial(kernel, gx_count, gy_count), out_shape=j...  42 us
    unnamed x1, local copies, waits for them, and re-layouts  1.57 us

profile of v1, /device:TPU:1, one launch (start us, length us, event | category | flops | bytes accessed | tf_op | source)
XLA Modules:
  0.0 44.3 jit_solution(14427103445471580255)
XLA Ops:
  0.7 42.0 %vcycle.1 = f32[2,128,128]{2,1,0:T(8,128)} custom-call(f32[2,128,128]{2,1,0:T(8,128)} %rhs_hbm.1, f32[128,128]{1,0:T(8,128)} %shift_hbm.1, f32[128,128]{1,0:T(8,128)} %visc_hbm.1, s32[1,1]{1,0:T(1,128)S(6)} %copy.6.wet_ref), custom_call_target="tpu_custom_call" | custom-call | tf_op jit(solution)/shard_map/vcycle/pallas_call | solution.py:486
  42.7 1.6 %copy.7 = f32[2,128,128]{2,1,0:T(8,128)} copy(f32[2,128,128]{2,1,0:T(8,128)} %vcycle.1) | data formatting | bytes 262144

commit v2 on v1

v2 whole, which is shorter than its diff:
```python
import functools

import jax
import jax.numpy as jnp
from jax import lax
from jax.experimental import pallas as pl
from jax.experimental.pallas import tpu as pltpu
from jax.sharding import PartitionSpec as P

TILE = 128
OMEGA = 0.8
KEEP = 1.0 - OMEGA
HALO = 24
ROWS = TILE + 2 * HALO
PAD = 8
F32 = jnp.float32
MESH = pl.DeviceIdType.MESH
DIRECTIONS = ((-1, 0), (1, 0), (0, -1), (0, 1), (-1, -1), (-1, 1), (1, -1), (1, 1))


def iota(shape, dim):
    return lax.broadcasted_iota(jnp.int32, shape, dim)


def roll_rows(x, k):
    return pltpu.roll(x, k % x.shape[0], axis=0)


def roll_lanes(x, k):
    return pltpu.roll(x, k % x.shape[1], axis=1)


def exact_dot(a, b, transposed=False):
    dims = (((1,), (1,)), ((), ())) if transposed else (((1,), (0,)), ((), ()))
    return lax.dot_general(
        a, b, dims, precision=lax.Precision.HIGHEST, preferred_element_type=F32
    )


def coefficients(viscous, reaction, level, pitch, closed=None):
    spacing = 0.25**level
    up = jnp.minimum(viscous, roll_rows(viscous, 1)) * spacing
    left = jnp.minimum(viscous, roll_lanes(viscous, pitch)) * spacing
    if closed is not None:
        up = jnp.where(closed[0], 0.0, up)
        left = jnp.where(closed[1], 0.0, left)
    down = roll_rows(up, -1)
    right = roll_lanes(left, -pitch)
    weight = OMEGA / (reaction + ((up + down) + (left + right)))
    return up, down, left, right, weight


def inflow(iterate, faces, pitch):
    up, down, left, right = faces[:4]
    return (up * roll_rows(iterate, 1) + down * roll_rows(iterate, -1)) + (
        left * roll_lanes(iterate, pitch) + right * roll_lanes(iterate, -pitch)
    )


def residual_of(source, iterate, faces, pitch):
    return KEEP * source + inflow(iterate, faces, pitch)


def swept(source, iterate, faces, pitch):
    return KEEP * iterate + faces[4] * (source + inflow(iterate, faces, pitch))


def kernel(
    gx_count,
    gy_count,
    rhs_hbm,
    shift_hbm,
    visc_hbm,
    wet_hbm,
    out_ref,
    own,
    wet_ref,
    strips,
    row_halo,
    col_halo,
    corner_halo,
    column_coef,
    column_source,
    gy_coef,
    gy_source,
    ext,
    pooled,
    level0,
    level1,
    level2,
    level3,
    stacked,
    spread,
    coarse,
    load_sem,
    halo_send,
    halo_recv,
    coef_send,
    coef_recv,
    source_send,
    source_recv,
    gather_send,
    gather_recv,
):
    a = lax.axis_index("gx")
    b = lax.axis_index("gy")
    has_up, has_down = a > 0, a < gx_count - 1
    has_left, has_right = b > 0, b < gy_count - 1
    has_row = {-1: has_up, 1: has_down}
    has_col = {-1: has_left, 1: has_right}

    def exists(da, db):
        if da == 0:
            return has_col[db]
        if db == 0:
            return has_row[da]
        return jnp.logical_and(has_row[da], has_col[db])

    loads = [
        pltpu.make_async_copy(wet_hbm, wet_ref, load_sem.at[3]),
        pltpu.make_async_copy(visc_hbm, own.at[3], load_sem.at[2]),
        pltpu.make_async_copy(rhs_hbm, own.at[pl.ds(0, 2)], load_sem.at[0]),
        pltpu.make_async_copy(shift_hbm, own.at[2], load_sem.at[1]),
    ]
    for load in loads:
        load.start()

    barrier = pltpu.get_barrier_semaphore()

    def greet(da, db):
        peer = (lax.rem(a + da, gx_count), lax.rem(b + db + gy_count, gy_count))
        pl.semaphore_signal(barrier, inc=1, device_id=peer, device_id_type=MESH)

    def greet_column(db):
        def one(k, carry):
            greet(k, db)
            return carry

        lax.fori_loop(1, gx_count, one, 0)

    def greet_row(k, carry):
        greet(0, k)
        return carry

    pl.when(has_left)(lambda: greet_column(-1))
    pl.when(has_right)(lambda: greet_column(1))
    greet_column(0)
    lax.fori_loop(1, gy_count, greet_row, 0)

    for f in range(4):
        for t in range(2):
            edge = jnp.full((PAD, 128), 1.0 if f == 2 else 0.0, F32)
            pooled[f, t, 0:PAD, :] = edge
            pooled[f, t, PAD + ROWS :, :] = edge
    for load in loads:
        load.wait()

    wet = wet_ref[0, 0].astype(F32)
    for f in (0, 1, 3):
        own[f] = own[f] * wet

    slot = iota((TILE, 128), 1) // 32
    for side, first in ((0, 0), (1, TILE - HALO)):
        packed = roll_lanes(own[0], -first)
        for f in range(1, 4):
            packed = jnp.where(slot == f, roll_lanes(own[f], f * 32 - first), packed)
        strips[side] = packed

    columns = jnp.where(has_left, 1, 0) + jnp.where(has_right, 1, 0) + 1
    pl.semaphore_wait(barrier, columns * (gx_count - 1) + gy_count - 1)

    def remote(src, dst, send_sem, recv_sem, da, db):
        peer = (lax.rem(a + da + gx_count, gx_count), lax.rem(b + db + gy_count, gy_count))
        return pltpu.make_async_remote_copy(
            src_ref=src,
            dst_ref=dst,
            send_sem=send_sem,
            recv_sem=recv_sem,
            device_id=peer,
            device_id_type=MESH,
        )

    halo_copies = []
    for i, (da, db) in enumerate(DIRECTIONS):
        first = 0 if da < 0 else TILE - HALO
        if db == 0:
            src, dst = own.at[:, pl.ds(first, HALO)], row_halo.at[i]
        elif da == 0:
            src, dst = strips.at[0 if db < 0 else 1], col_halo.at[i - 2]
        else:
            src = strips.at[0 if db < 0 else 1, pl.ds(first, HALO)]
            dst = corner_halo.at[i - 4]
        copy = remote(src, dst, halo_send.at[i], halo_recv.at[i], da, db)
        halo_copies.append(copy)
    for i in (4, 5, 6, 7, 2, 3, 0, 1):
        pl.when(exists(*DIRECTIONS[i]))(halo_copies[i].start)

    gx_order = sorted(range(1, gx_count), key=lambda k: -min(k, gx_count - k))

    def column_copies(slots, sends, recvs, db):
        def copy(k):
            return remote(
                slots.at[1, a], slots.at[1 - db, a], sends.at[db + 1], recvs.at[1 - db], k, db
            )

        ks = gx_order if db == 0 else [*gx_order, 0]
        return [copy(k) for k in ks]

    def start_columns(slots, sends, recvs):
        for db in (-1, 1, 0):
            copies = column_copies(slots, sends, recvs, db)

            def start(copies=copies):
                for copy in copies:
                    copy.start()

            if db == 0:
                start()
            else:
                pl.when(has_col[db])(start)

    def finish_columns(slots, sends, recvs):
        for db in (-1, 1, 0):
            count = gx_count - 1 if db == 0 else gx_count
            every = remote(
                slots.at[1 - db, pl.ds(0, count)],
                slots.at[1 - db, pl.ds(0, count)],
                sends.at[db + 1],
                recvs.at[1 + db],
                1,
                0,
            )
            if db == 0:
                every.wait()
            else:
                pl.when(has_col[db])(every.wait)

    lane8 = iota((8, 128), 1)
    own_column = lane8 // 16 == iota((8, 128), 0)
    average = jnp.where(own_column, 0.0625, 0.0)
    to_lane = iota((128, 128), 1)
    from_row = iota((128, 128), 0)
    total = jnp.zeros((8, 128), F32)
    for f in range(2):
        to_row = jnp.where(
            (from_row // 16 == to_lane % 8) & (to_lane // 8 % 2 == f), 0.0625, 0.0
        )
        total = total + exact_dot(exact_dot(average, own[2 + f], True), to_row)

    def one_row(x):
        mine = jnp.where(lane8 // 16 == 7 - iota((8, 128), 0), x, 0.0)
        turned = pltpu.roll(mine, lax.rem(8 * a + 8, 128), axis=1)
        return jnp.sum(turned, axis=0, keepdims=True)

    column_coef[1, a] = one_row(total)
    start_columns(column_coef, coef_send, coef_recv)

    for f in range(4):
        ext[f, HALO : HALO + TILE, 0:128] = own[f]
    for i, (da, db) in enumerate(DIRECTIONS):
        pl.when(exists(da, db))(halo_copies[i].wait_send)
        pl.when(exists(-da, -db))(halo_copies[i].wait_recv)

    lane = iota((1, 128), 1)
    all_up = lane < jnp.where(has_up, 128, 0)
    all_down = lane < jnp.where(has_down, 128, 0)
    beside = (lane < jnp.where(has_right, HALO, 0)) | (
        lane >= jnp.where(has_left, TILE - HALO, 128)
    )
    for f in range(4):
        fill = 1.0 if f == 2 else 0.0
        ext[f, 0:HALO, 0:128] = jnp.where(all_up, row_halo[1, f], fill)
        ext[f, HALO + TILE :, 0:128] = jnp.where(all_down, row_halo[0, f], fill)

        def side(right, left, valid):
            r = roll_lanes(right, -f * 32)
            l = roll_lanes(left, TILE - HALO - f * 32)
            return jnp.where(valid, jnp.where(lane < 64, r, l), fill)

        ext[f, HALO : HALO + TILE, 128:256] = side(col_halo[0], col_halo[1], beside)
        ext[f, 0:HALO, 128:256] = side(corner_halo[2], corner_halo[3], beside & all_up)
        ext[f, HALO + TILE :, 128:256] = side(corner_halo[0], corner_halo[1], beside & all_down)

    def pool(x, i, pitch, first=0, start=0, rows=None):
        n = x.shape[0]
        width = x.shape[1]
        rows = n // 2 if rows is None else rows
        parts = []
        for t in range(width // 128):
            pooled[i, t, first : first + n, :] = x[:, t * 128 : t * 128 + 128]
            parts.append(
                pooled[i, t, pl.ds(start, rows, stride=2), :]
                + pooled[i, t, pl.ds(start + 1, rows, stride=2), :]
            )
        y = parts[0] if len(parts) == 1 else jnp.concatenate(parts, axis=1)
        return y if pitch is None else (y + roll_lanes(y, -pitch)) * 0.25

    fields = [ext[f] for f in range(4)]
    stores = (level0, level1, level2, level3)
    for level in range(4):
        pitch = 2**level
        keep = stores[level]
        faces = coefficients(fields[3], fields[2], level, pitch)
        for j in range(5):
            keep[j] = faces[j]
        residuals = []
        for c in range(2):
            iterate = fields[c] * faces[4]
            keep[5 + c] = fields[c]
            residuals.append(residual_of(fields[c], iterate, faces, pitch))
        if level < 3:
            shape = (PAD, 0, (ROWS + 2 * PAD) // 2) if level == 0 else (0, 0, None)
            fields = [
                pool(x, i, pitch, *shape)
                for i, x in enumerate((*residuals, fields[2], fields[3]))
            ]

    for c in range(2):
        half = pool(residuals[c][:, 0:128], c, None, 0, 4, 8)
        for j in range(8):
            stacked[j * 16 + c * 8 : j * 16 + c * 8 + 8, :] = half
    pick = jnp.where(own_column & (lane8 % 8 == 0), 0.25, 0.0)
    column_source[1, a] = one_row(exact_dot(pick, stacked[...], True))
    start_columns(column_source, source_send, source_recv)

    def assembled(slots, fills):
        parts = ([], [])
        for col in range(3):
            for t in range(2):
                block = jnp.zeros((8, 128), F32)
                for j in range(gx_count):
                    row = jnp.broadcast_to(slots[col, j], (8, 128))
                    moved = pltpu.roll(
                        row, 8 - t * 8, axis=1, stride=16, stride_axis=0
                    )
                    block = jnp.where(lane8 // 8 == j, moved, block)
                if gx_count < 16:
                    block = jnp.where(lane8 // 8 < gx_count, block, fills[t])
                if col != 1:
                    limit = jnp.where(has_left if col == 0 else has_right, 128, 0)
                    block = jnp.where(lane8 < limit, block, fills[t])
                parts[t].append(block)
        return [
            jnp.concatenate([*parts[t], jnp.full((8, 128), fills[t], F32)], axis=0)
            for t in range(2)
        ]

    def closed_rows(shape, pitch, columns_too):
        first_col = iota(shape, 0) == (0 if columns_too else -1)
        return first_col, iota(shape, 1) < pitch

    finish_columns(column_coef, coef_send, coef_recv)
    reaction, viscous = assembled(column_coef, (1.0, 0.0))
    mid_faces = []
    for level in (4, 5):
        pitch = 2 ** (level - 4)
        closed = closed_rows(viscous.shape, pitch, False)
        mid_faces.append(coefficients(viscous, reaction, level, pitch, closed))
        reaction, viscous = pool(reaction, 2, pitch), pool(viscous, 3, pitch)

    def level6_row(x, y):
        x, y = jnp.where(lane8 % 4 == 0, x, 0.0), jnp.where(lane8 % 4 == 0, y, 0.0)
        both = x + roll_lanes(y, 1)
        return both[2:3] + roll_lanes(both[3:4], 2)

    def hops(k):
        x, y = k // 8, k % 8
        return min(x, 4 - x) + min(y, 8 - y)

    gy_order = sorted(range(1, gy_count), key=lambda k: -hops(k))

    def start_row(slots, sem):
        for k in gy_order:
            remote(slots.at[b], slots.at[b], gather_send.at[sem], gather_recv.at[sem], 0, k).start()

    def finish_row(slots, sem):
        rest = slots.at[pl.ds(0, gy_count - 1)]
        remote(rest, rest, gather_send.at[sem], gather_recv.at[sem], 0, 1).wait()

    gy_coef[b, 0:1, :] = level6_row(reaction, reaction)
    gy_coef[b, 1:2, :] = level6_row(viscous, viscous)
    start_row(gy_coef, 0)

    finish_columns(column_source, source_send, source_recv)
    source4 = assembled(column_source, (0.0, 0.0))
    source5 = [
        pool(residual_of(x, x * mid_faces[0][4], mid_faces[0], 1), c, 1)
        for c, x in enumerate(source4)
    ]
    source6 = [
        pool(residual_of(x, x * mid_faces[1][4], mid_faces[1], 2), c, 2)
        for c, x in enumerate(source5)
    ]
    gy_source[b] = level6_row(*source6)
    start_row(gy_source, 1)

    def spread_rows(x, i=0):
        n = x.shape[0]
        parts = []
        for t in range(x.shape[1] // 128):
            piece = x[:, t * 128 : t * 128 + 128]
            spread[i, t, pl.ds(0, n, stride=2), :] = piece
            spread[i, t, pl.ds(1, n, stride=2), :] = piece
            start = PAD if 2 * n > ROWS else 0
            parts.append(spread[i, t, start : 2 * n - start, :])
        return parts[0] if len(parts) == 1 else jnp.concatenate(parts, axis=1)

    def widened(x, pitch, i=0):
        odd = (iota((1, x.shape[1]), 1) & pitch) != 0
        return spread_rows(jnp.where(odd, roll_lanes(x, pitch), x), i)

    cols6 = 64

    def whole(read, i):
        for j in range(gy_count):
            coarse[i, 64 + j : 65 + j, :] = read(j)
        rows = coarse[i, 64:96, :]
        coarse[i, pl.ds(0, 32, stride=2), :] = rows
        coarse[i, pl.ds(1, 32, stride=2), :] = roll_lanes(rows, -2)
        return coarse[i, 0:cols6, :]

    if gy_count * 2 < cols6:
        coarse[...] = jnp.zeros_like(coarse)

    finish_row(gy_coef, 0)
    reaction = whole(lambda j: gy_coef[j, 0:1, :], 0)
    viscous = whole(lambda j: gy_coef[j, 1:2, :], 1)
    if gx_count * 2 < 32 or gy_count * 2 < cols6:
        reaction = jnp.where(reaction == 0.0, 1.0, reaction)
    coarse_faces = []
    for level in range(6, 9):
        pitch = 2 ** (level - 4)
        closed = closed_rows(viscous.shape, pitch, True)
        coarse_faces.append(coefficients(viscous, reaction, level, pitch, closed))
        if level < 8:
            reaction, viscous = pool(reaction, 2, pitch), pool(viscous, 3, pitch)
    up, down, left, right, weight8 = coarse_faces[2]
    scaled8 = (weight8 * up, weight8 * down, weight8 * left, weight8 * right)

    take_cols = jnp.where(
        iota((16, cols6), 1) == 2 * b - 2 + iota((16, cols6), 0) // 2, 1.0, 0.0
    )
    rows_back = jnp.where(
        iota((24, 128), 1) == 8 * a + (iota((24, 128), 0) + 4) // 2 - 4, 1.0, 0.0
    )
    fine = iota((32, 256), 1)
    fine = jnp.where(fine < 192, fine + 256, fine)
    cols_back = jnp.where(iota((32, 256), 0) == fine // 16 - 8, 1.0, 0.0)

    finish_row(gy_source, 1)
    source = whole(lambda j: gy_source[j], 2)
    coarse_sources = []
    for level in (6, 7):
        pitch = 2 ** (level - 4)
        faces = coarse_faces[level - 6]
        coarse_sources.append(source)
        source = pool(residual_of(source, source * faces[4], faces, pitch), 0, pitch)
    start = weight8 * source
    now = start
    for _ in range(7):
        now = (KEEP * now + start) + inflow(now, scaled8, 16)
    for level in (7, 6):
        pitch = 2 ** (level - 4)
        faces = coarse_faces[level - 6]
        source = coarse_sources[level - 6]
        now = swept(source, source * faces[4] + widened(now, pitch), faces, pitch)

    near = exact_dot(take_cols, now)
    lane16 = iota((16, 128), 1)
    current = []
    for c in range(2):
        mine = jnp.where(lane16 % 4 == c, near, 0.0)
        mine = roll_lanes(mine, -c) if c else mine
        correction = mine + roll_lanes(mine, 2)
        x = source5[c]
        result = swept(x, x * mid_faces[1][4] + correction, mid_faces[1], 2)
        x = source4[c]
        result = swept(x, x * mid_faces[0][4] + widened(result, 1, c), mid_faces[0], 1)
        current.append(exact_dot(exact_dot(rows_back, result, True), cols_back))

    for level in (3, 2, 1, 0):
        pitch = 2**level
        keep = stores[level]
        faces = [keep[j] for j in range(5)]
        for c in range(2):
            source = keep[5 + c]
            correction = current[c] if level == 3 else widened(current[c], pitch, c)
            result = swept(source, source * faces[4] + correction, faces, pitch)
            if level == 0:
                out_ref[c] = result[HALO : HALO + TILE, 0:128]
            else:
                current[c] = result


def solution(mesh):
    gx_count, gy_count = mesh.shape["gx"], mesh.shape["gy"]

    def per_device(right_side, shift_coef, viscosity, wet_tiles):
        hbm = pl.BlockSpec(memory_space=pltpu.HBM)
        dma = pltpu.SemaphoreType.DMA
        inner = (ROWS + 2 * PAD) // 2
        return pl.pallas_call(
            functools.partial(kernel, gx_count, gy_count),
            out_shape=pltpu.VMEM((2, TILE, TILE), F32),
            in_specs=[hbm, hbm, hbm, hbm],
            out_specs=pl.BlockSpec(memory_space=pltpu.VMEM),
            scratch_shapes=[
                pltpu.VMEM((4, TILE, TILE), F32),
                pltpu.SMEM((1, 1), jnp.int32),
                pltpu.VMEM((2, TILE, 128), F32),
                pltpu.VMEM((2, 4, HALO, 128), F32),
                pltpu.VMEM((2, TILE, 128), F32),
                pltpu.VMEM((4, HALO, 128), F32),
                pltpu.VMEM((3, gx_count, 1, 128), F32),
                pltpu.VMEM((3, gx_count, 1, 128), F32),
                pltpu.VMEM((gy_count, 2, 128), F32),
                pltpu.VMEM((gy_count, 1, 128), F32),
                pltpu.VMEM((4, ROWS, 256), F32),
                pltpu.VMEM((4, 2, ROWS + 2 * PAD, 128), F32),
                pltpu.VMEM((7, ROWS, 256), F32),
                pltpu.VMEM((7, inner, 256), F32),
                pltpu.VMEM((7, inner // 2, 256), F32),
                pltpu.VMEM((7, inner // 4, 256), F32),
                pltpu.VMEM((128, 128), F32),
                pltpu.VMEM((2, 2, ROWS + 2 * PAD, 128), F32),
                pltpu.VMEM((3, 96, 128), F32),
                dma((4,)),
                dma((8,)),
                dma((8,)),
                dma((3,)),
                dma((3,)),
                dma((3,)),
                dma((3,)),
                dma((2,)),
                dma((2,)),
            ],
            compiler_params=pltpu.CompilerParams(collective_id=0, has_side_effects=True),
            name="vcycle",
        )(right_side, shift_coef, viscosity, wet_tiles)

    placed = (P(None, "gx", "gy"), P("gx", "gy"), P("gx", "gy"), P("gx", "gy"))
    return jax.shard_map(
        per_device, mesh=mesh, in_specs=placed, out_specs=P(None, "gx", "gy"), check_vma=False
    )
```

time: 44.4 us -> 38.1 us (0.86)
  Pallas kernels: 42 us -> 36.7 us
  local copies, waits for them, and re-layouts: 1.57 us -> 0.66 us
    pallas_call x1, Pallas kernels: 42 us -> 36.7 us  [per_device(): pl.pallas_call(functools.partial(kernel, gx_count, gy_count), out_shape=p...]
    unnamed x1, local copies, waits for them, and re-layouts: 1.57 us -> 0.66 us
where the time goes in v2:
time: 38.1 us; the launch traced here: 38 us
  Pallas kernels  36.7 us (96%)
  local copies, waits for them, and re-layouts  0.66 us (2%)
  between operations  0.66 us (2%)
    pallas_call x1, Pallas kernels, per_device(): pl.pallas_call(functools.partial(kernel, gx_count, gy_count), out_shape=p...  36.7 us

profile of v2, /device:TPU:1, one launch (start us, length us, event | category | flops | bytes accessed | tf_op | source)
XLA Modules:
  0.0 38.0 jit_solution(8423201501514221319)
XLA Ops:
  0.7 36.7 %vcycle.1 = f32[2,128,128]{2,1,0:T(8,128)S(1)} custom-call(f32[2,128,128]{2,1,0:T(8,128)} %rhs_hbm.1, f32[128,128]{1,0:T(8,128)} %shift_hbm.1, f32[128,128]{1,0:T(8,128)} %visc_hbm.1, s32[1,1]{1,0:T(1,128)S(6)} %copy.7.wet_hbm), custom_call_target="tpu_custom_call" | custom-call | tf_op jit(solution)/shard_map/vcycle/pallas_call | solution.py:502
  37.4 0.7 %copy.6 = f32[2,128,128]{2,1,0:T(8,128)} copy(f32[2,128,128]{2,1,0:T(8,128)S(1)} %vcycle.1) | data formatting | bytes 262144

commit v3 on v2

--- a/solution.py
+++ b/solution.py
@@ -101,6 +101,7 @@
     source_recv,
     gather_send,
     gather_recv,
+    known,
 ):
     a = lax.axis_index("gx")
     b = lax.axis_index("gy")
@@ -115,6 +116,14 @@
         if db == 0:
             return has_row[da]
         return jnp.logical_and(has_row[da], has_col[db])
+
+    barrier = pltpu.get_barrier_semaphore()
+
+    def around(da, db):
+        return (lax.rem(a + da + gx_count, gx_count), lax.rem(b + db + gy_count, gy_count))
+
+    for da, db in DIRECTIONS[4:] + DIRECTIONS[:4]:
+        pl.semaphore_signal(barrier, inc=1, device_id=around(da, db), device_id_type=MESH)
 
     loads = [
         pltpu.make_async_copy(wet_hbm, wet_ref, load_sem.at[3]),
@@ -125,27 +134,22 @@
     for load in loads:
         load.start()
 
-    barrier = pltpu.get_barrier_semaphore()
-
-    def greet(da, db):
-        peer = (lax.rem(a + da, gx_count), lax.rem(b + db + gy_count, gy_count))
-        pl.semaphore_signal(barrier, inc=1, device_id=peer, device_id_type=MESH)
-
-    def greet_column(db):
-        def one(k, carry):
-            greet(k, db)
-            return carry
-
-        lax.fori_loop(1, gx_count, one, 0)
-
-    def greet_row(k, carry):
-        greet(0, k)
-        return carry
-
-    pl.when(has_left)(lambda: greet_column(-1))
-    pl.when(has_right)(lambda: greet_column(1))
-    greet_column(0)
-    lax.fori_loop(1, gy_count, greet_row, 0)
+    reach = {"gx": 1, "gy": 1}
+
+    def tell(axis):
+        r, count = reach[axis], gx_count if axis == "gx" else gy_count
+        if r < count // 2:
+            sem = known.at[(0 if axis == "gx" else 8) + r.bit_length()]
+            for step in (r, -r):
+                peer = around(step, 0) if axis == "gx" else around(0, step)
+                pl.semaphore_signal(sem, inc=1, device_id=peer, device_id_type=MESH)
+
+    def hear(axis):
+        r, count = reach[axis], gx_count if axis == "gx" else gy_count
+        if r < count // 2:
+            sem = known.at[(0 if axis == "gx" else 8) + r.bit_length()]
+            pl.semaphore_wait(sem, 2)
+            reach[axis] = 2 * r
 
     for f in range(4):
         for t in range(2):
@@ -166,17 +170,15 @@
             packed = jnp.where(slot == f, roll_lanes(own[f], f * 32 - first), packed)
         strips[side] = packed
 
-    columns = jnp.where(has_left, 1, 0) + jnp.where(has_right, 1, 0) + 1
-    pl.semaphore_wait(barrier, columns * (gx_count - 1) + gy_count - 1)
+    pl.semaphore_wait(barrier, 8)
 
     def remote(src, dst, send_sem, recv_sem, da, db):
-        peer = (lax.rem(a + da + gx_count, gx_count), lax.rem(b + db + gy_count, gy_count))
         return pltpu.make_async_remote_copy(
             src_ref=src,
             dst_ref=dst,
             send_sem=send_sem,
             recv_sem=recv_sem,
-            device_id=peer,
+            device_id=around(da, db),
             device_id_type=MESH,
         )
 
@@ -194,6 +196,8 @@
         halo_copies.append(copy)
     for i in (4, 5, 6, 7, 2, 3, 0, 1):
         pl.when(exists(*DIRECTIONS[i]))(halo_copies[i].start)
+    tell("gx")
+    tell("gy")
 
     gx_order = sorted(range(1, gx_count), key=lambda k: -min(k, gx_count - k))
 
@@ -253,10 +257,15 @@
         return jnp.sum(turned, axis=0, keepdims=True)
 
     column_coef[1, a] = one_row(total)
-    start_columns(column_coef, coef_send, coef_recv)
+    hear("gx")
+    tell("gx")
+    hear("gy")
+    tell("gy")
 
     for f in range(4):
         ext[f, HALO : HALO + TILE, 0:128] = own[f]
+    hear("gx")
+    tell("gx")
     for i, (da, db) in enumerate(DIRECTIONS):
         pl.when(exists(da, db))(halo_copies[i].wait_send)
         pl.when(exists(-da, -db))(halo_copies[i].wait_recv)
@@ -308,6 +317,13 @@
             iterate = fields[c] * faces[4]
             keep[5 + c] = fields[c]
             residuals.append(residual_of(fields[c], iterate, faces, pitch))
+        if level == 0:
+            hear("gy")
+            tell("gy")
+        if level == 1:
+            hear("gx")
+            assert reach["gx"] >= gx_count // 2
+            start_columns(column_coef, coef_send, coef_recv)
         if level < 3:
             shape = (PAD, 0, (ROWS + 2 * PAD) // 2) if level == 0 else (0, 0, None)
             fields = [
@@ -322,6 +338,8 @@
     pick = jnp.where(own_column & (lane8 % 8 == 0), 0.25, 0.0)
     column_source[1, a] = one_row(exact_dot(pick, stacked[...], True))
     start_columns(column_source, source_send, source_recv)
+    hear("gy")
+    tell("gy")
 
     def assembled(slots, fills):
         parts = ([], [])
@@ -377,6 +395,8 @@
         rest = slots.at[pl.ds(0, gy_count - 1)]
         remote(rest, rest, gather_send.at[sem], gather_recv.at[sem], 0, 1).wait()
 
+    hear("gy")
+    assert reach["gy"] >= gy_count // 2
     gy_coef[b, 0:1, :] = level6_row(reaction, reaction)
     gy_coef[b, 1:2, :] = level6_row(viscous, viscous)
     start_row(gy_coef, 0)
@@ -533,6 +553,7 @@
                 dma((3,)),
                 dma((2,)),
                 dma((2,)),
+                pltpu.SemaphoreType.REGULAR((16,)),
             ],
             compiler_params=pltpu.CompilerParams(collective_id=0, has_side_effects=True),
             name="vcycle",

time: 38.1 us -> 36.2 us (0.950)
  Pallas kernels: 36.7 us -> 34.7 us
    pallas_call x1, Pallas kernels: 36.7 us -> 34.7 us  [per_device(): pl.pallas_call(functools.partial(kernel, gx_count, gy_count), out_shape=p...]
where the time goes in v3:
time: 36.2 us; the launch traced here: 36.1 us
  Pallas kernels  34.7 us (96%)
  local copies, waits for them, and re-layouts  0.66 us (2%)
  between operations  0.66 us (2%)
    pallas_call x1, Pallas kernels, per_device(): pl.pallas_call(functools.partial(kernel, gx_count, gy_count), out_shape=p...  34.7 us

profile of v3, /device:TPU:1, one launch (start us, length us, event | category | flops | bytes accessed | tf_op | source)
XLA Modules:
  0.0 36.1 jit_solution(11336852759525455917)
XLA Ops:
  0.7 34.7 %vcycle.1 = f32[2,128,128]{2,1,0:T(8,128)S(1)} custom-call(f32[2,128,128]{2,1,0:T(8,128)} %rhs_hbm.1, f32[128,128]{1,0:T(8,128)} %shift_hbm.1, f32[128,128]{1,0:T(8,128)} %visc_hbm.1, s32[1,1]{1,0:T(1,128)S(6)} %copy.7.wet_hbm), custom_call_target="tpu_custom_call" | custom-call | tf_op jit(solution)/shard_map/vcycle/pallas_call | solution.py:522
  35.4 0.7 %copy.6 = f32[2,128,128]{2,1,0:T(8,128)} copy(f32[2,128,128]{2,1,0:T(8,128)S(1)} %vcycle.1) | data formatting | bytes 262144

commit v4 on v3

--- a/solution.py
+++ b/solution.py
@@ -35,6 +35,20 @@
     return lax.dot_general(
         a, b, dims, precision=lax.Precision.HIGHEST, preferred_element_type=F32
     )
+
+
+def picked(x, one_hot, left=False):
+    total = None
+    for _ in range(3):
+        piece = x.astype(jnp.bfloat16)
+        x = x - piece.astype(F32)
+        if left:
+            dims, pair = (((1,), (1,)), ((), ())), (one_hot, piece)
+        else:
+            dims, pair = (((1,), (0,)), ((), ())), (piece, one_hot)
+        part = lax.dot_general(*pair, dims, preferred_element_type=F32)
+        total = part if total is None else total + part
+    return total
 
 
 def coefficients(viscous, reaction, level, pitch, closed=None):
@@ -59,6 +73,14 @@
 
 def residual_of(source, iterate, faces, pitch):
     return KEEP * source + inflow(iterate, faces, pitch)
+
+
+def scaled(faces):
+    return tuple(faces[4] * face for face in faces[:4])
+
+
+def corrected(base, correction, faces, pitch):
+    return (base + KEEP * correction) + inflow(correction, faces, pitch)
 
 
 def swept(source, iterate, faces, pitch):
@@ -92,6 +114,7 @@
     stacked,
     spread,
     coarse,
+    final,
     load_sem,
     halo_send,
     halo_recv,
@@ -201,27 +224,27 @@
 
     gx_order = sorted(range(1, gx_count), key=lambda k: -min(k, gx_count - k))
 
-    def column_copies(slots, sends, recvs, db):
-        def copy(k):
-            return remote(
-                slots.at[1, a], slots.at[1 - db, a], sends.at[db + 1], recvs.at[1 - db], k, db
-            )
-
-        ks = gx_order if db == 0 else [*gx_order, 0]
-        return [copy(k) for k in ks]
-
     def start_columns(slots, sends, recvs):
-        for db in (-1, 1, 0):
-            copies = column_copies(slots, sends, recvs, db)
-
-            def start(copies=copies):
-                for copy in copies:
-                    copy.start()
-
-            if db == 0:
-                start()
-            else:
-                pl.when(has_col[db])(start)
+        half = gx_count // 2
+        for part in (slice(0, half), slice(half, gx_count)):
+            for db in (-1, 1, 0):
+                ks = [*gx_order, 0][part] if db else gx_order[part]
+
+                def start(ks=ks, db=db):
+                    for k in ks:
+                        remote(
+                            slots.at[1, a],
+                            slots.at[1 - db, a],
+                            sends.at[db + 1],
+                            recvs.at[1 - db],
+                            k,
+                            db,
+                        ).start()
+
+                if db == 0:
+                    start()
+                else:
+                    pl.when(has_col[db])(start)
 
     def finish_columns(slots, sends, recvs):
         for db in (-1, 1, 0):
@@ -303,6 +326,10 @@
             )
         y = parts[0] if len(parts) == 1 else jnp.concatenate(parts, axis=1)
         return y if pitch is None else (y + roll_lanes(y, -pitch)) * 0.25
+
+    turned_row = lax.rem(iota((128, 128), 0) + (256 - 8 - 8 * a), 128)
+    pairs = (to_lane // 16 == 7 - turned_row // 16) & (to_lane % 8 == 0)
+    quarter = jnp.full((8, 128), 0.25, jnp.bfloat16)
 
     fields = [ext[f] for f in range(4)]
     stores = (level0, level1, level2, level3)
@@ -334,10 +361,28 @@
     for c in range(2):
         half = pool(residuals[c][:, 0:128], c, None, 0, 4, 8)
         for j in range(8):
-            stacked[j * 16 + c * 8 : j * 16 + c * 8 + 8, :] = half
-    pick = jnp.where(own_column & (lane8 % 8 == 0), 0.25, 0.0)
-    column_source[1, a] = one_row(exact_dot(pick, stacked[...], True))
+            place = lax.rem(8 * a + (j * 16 + c * 8 + 8), 128)
+            stacked[pl.ds(pl.multiple_of(place, 8), 8), :] = half
+    paired = jnp.where(pairs, stacked[...], 0.0)
+    column_source[1, a] = picked(paired, quarter, True)[0:1]
     start_columns(column_source, source_send, source_recv)
+
+    inside = slice(HALO, HALO + TILE)
+    for level in range(4):
+        pitch = 2**level
+        keep = stores[level]
+        faces = [keep[j] for j in range(5)]
+        for c in range(2):
+            base = swept(keep[5 + c], keep[5 + c] * faces[4], faces, pitch)
+            if level == 0:
+                final[4 + c] = base[inside, 0:128]
+            else:
+                keep[5 + c] = base
+        for j, face in enumerate(scaled(faces)):
+            if level == 0:
+                final[j] = face[inside, 0:128]
+            else:
+                keep[j] = face
     hear("gy")
     tell("gy")
 
@@ -378,8 +423,9 @@
 
     def level6_row(x, y):
         x, y = jnp.where(lane8 % 4 == 0, x, 0.0), jnp.where(lane8 % 4 == 0, y, 0.0)
-        both = x + roll_lanes(y, 1)
-        return both[2:3] + roll_lanes(both[3:4], 2)
+        first = x + roll_lanes(y, 1)
+        second = roll_lanes(x, 2) + roll_lanes(y, 3)
+        return first[2:3] + second[3:4]
 
     def hops(k):
         x, y = k // 8, k % 8
@@ -413,6 +459,9 @@
     ]
     gy_source[b] = level6_row(*source6)
     start_row(gy_source, 1)
+    base4 = [swept(x, x * mid_faces[0][4], mid_faces[0], 1) for x in source4]
+    base5 = [swept(x, x * mid_faces[1][4], mid_faces[1], 2) for x in source5]
+    scaled4, scaled5 = scaled(mid_faces[0]), scaled(mid_faces[1])
 
     def spread_rows(x, i=0):
         n = x.shape[0]
@@ -431,20 +480,17 @@
 
     cols6 = 64
 
-    def whole(read, i):
-        for j in range(gy_count):
-            coarse[i, 64 + j : 65 + j, :] = read(j)
-        rows = coarse[i, 64:96, :]
-        coarse[i, pl.ds(0, 32, stride=2), :] = rows
-        coarse[i, pl.ds(1, 32, stride=2), :] = roll_lanes(rows, -2)
-        return coarse[i, 0:cols6, :]
+    def whole(rows, i):
+        coarse[i, pl.ds(0, gy_count, stride=2), :] = rows
+        coarse[i, pl.ds(1, gy_count, stride=2), :] = roll_lanes(rows, -2)
+        return coarse[i]
 
     if gy_count * 2 < cols6:
         coarse[...] = jnp.zeros_like(coarse)
 
     finish_row(gy_coef, 0)
-    reaction = whole(lambda j: gy_coef[j, 0:1, :], 0)
-    viscous = whole(lambda j: gy_coef[j, 1:2, :], 1)
+    reaction = whole(gy_coef[:, 0, :], 0)
+    viscous = whole(gy_coef[:, 1, :], 1)
     if gx_count * 2 < 32 or gy_count * 2 < cols6:
         reaction = jnp.where(reaction == 0.0, 1.0, reaction)
     coarse_faces = []
@@ -454,62 +500,60 @@
         coarse_faces.append(coefficients(viscous, reaction, level, pitch, closed))
         if level < 8:
             reaction, viscous = pool(reaction, 2, pitch), pool(viscous, 3, pitch)
-    up, down, left, right, weight8 = coarse_faces[2]
-    scaled8 = (weight8 * up, weight8 * down, weight8 * left, weight8 * right)
-
-    take_cols = jnp.where(
-        iota((16, cols6), 1) == 2 * b - 2 + iota((16, cols6), 0) // 2, 1.0, 0.0
-    )
-    rows_back = jnp.where(
-        iota((24, 128), 1) == 8 * a + (iota((24, 128), 0) + 4) // 2 - 4, 1.0, 0.0
-    )
+    scaled8, weight8 = scaled(coarse_faces[2]), coarse_faces[2][4]
+    coarse_scaled = [scaled(faces) for faces in coarse_faces[:2]]
+
+    rows_back = iota((24, 128), 1) == 8 * a + (iota((24, 128), 0) + 4) // 2 - 4
+    rows_back = jnp.where(rows_back, 1.0, 0.0).astype(jnp.bfloat16)
     fine = iota((32, 256), 1)
     fine = jnp.where(fine < 192, fine + 256, fine)
-    cols_back = jnp.where(iota((32, 256), 0) == fine // 16 - 8, 1.0, 0.0)
+    cols_back = iota((32, 256), 0) == fine // 16 - 8
+    cols_back = jnp.where(cols_back, 1.0, 0.0).astype(jnp.bfloat16)
 
     finish_row(gy_source, 1)
-    source = whole(lambda j: gy_source[j], 2)
-    coarse_sources = []
+    source = whole(gy_source[:, 0, :], 2)
+    bases = []
     for level in (6, 7):
         pitch = 2 ** (level - 4)
         faces = coarse_faces[level - 6]
-        coarse_sources.append(source)
-        source = pool(residual_of(source, source * faces[4], faces, pitch), 0, pitch)
+        iterate = source * faces[4]
+        around_it = inflow(iterate, faces, pitch)
+        bases.append(KEEP * iterate + faces[4] * (source + around_it))
+        source = pool(KEEP * source + around_it, 0, pitch)
     start = weight8 * source
     now = start
     for _ in range(7):
-        now = (KEEP * now + start) + inflow(now, scaled8, 16)
+        now = corrected(start, now, scaled8, 16)
     for level in (7, 6):
         pitch = 2 ** (level - 4)
-        faces = coarse_faces[level - 6]
-        source = coarse_sources[level - 6]
-        now = swept(source, source * faces[4] + widened(now, pitch), faces, pitch)
-
-    near = exact_dot(take_cols, now)
+        now = corrected(bases[level - 6], widened(now, pitch), coarse_scaled[level - 6], pitch)
+
+    near = spread_rows(pltpu.roll(now, lax.rem(cols6 + 2 - 2 * b, cols6), axis=0)[0:8])
     lane16 = iota((16, 128), 1)
     current = []
     for c in range(2):
         mine = jnp.where(lane16 % 4 == c, near, 0.0)
         mine = roll_lanes(mine, -c) if c else mine
-        correction = mine + roll_lanes(mine, 2)
-        x = source5[c]
-        result = swept(x, x * mid_faces[1][4] + correction, mid_faces[1], 2)
-        x = source4[c]
-        result = swept(x, x * mid_faces[0][4] + widened(result, 1, c), mid_faces[0], 1)
-        current.append(exact_dot(exact_dot(rows_back, result, True), cols_back))
-
-    for level in (3, 2, 1, 0):
+        result = corrected(base5[c], mine + roll_lanes(mine, 2), scaled5, 2)
+        result = corrected(base4[c], widened(result, 1, c), scaled4, 1)
+        current.append(picked(picked(result, rows_back, True), cols_back))
+
+    for level in (3, 2, 1):
         pitch = 2**level
         keep = stores[level]
-        faces = [keep[j] for j in range(5)]
+        faces = [keep[j] for j in range(4)]
         for c in range(2):
-            source = keep[5 + c]
             correction = current[c] if level == 3 else widened(current[c], pitch, c)
-            result = swept(source, source * faces[4] + correction, faces, pitch)
-            if level == 0:
-                out_ref[c] = result[HALO : HALO + TILE, 0:128]
-            else:
-                current[c] = result
+            current[c] = corrected(keep[5 + c], correction, faces, pitch)
+
+    for c in range(2):
+        correction = widened(current[c], 1, c)
+        here, beyond = correction[:, 0:128], correction[inside, 128:256]
+        own_rows = here[inside]
+        before = jnp.where(lane == 0, roll_lanes(beyond, 1), roll_lanes(own_rows, 1))
+        after = jnp.where(lane == 127, roll_lanes(beyond, -1), roll_lanes(own_rows, -1))
+        rows = (final[0] * roll_rows(here, 1)[inside] + final[1] * roll_rows(here, -1)[inside])
+        out_ref[c] = (final[4 + c] + KEEP * own_rows) + (rows + (final[2] * before + final[3] * after))
 
 
 def solution(mesh):
@@ -543,7 +587,8 @@
                 pltpu.VMEM((7, inner // 4, 256), F32),
                 pltpu.VMEM((128, 128), F32),
                 pltpu.VMEM((2, 2, ROWS + 2 * PAD, 128), F32),
-                pltpu.VMEM((3, 96, 128), F32),
+                pltpu.VMEM((3, 64, 128), F32),
+                pltpu.VMEM((6, TILE, TILE), F32),
                 dma((4,)),
                 dma((8,)),
                 dma((8,)),

time: 36.2 us -> 36 us (level)
  no operation moved by 1% of the time
where the time goes in v4:
time: 36 us; the launch traced here: 35.9 us
  Pallas kernels  34.6 us (96%)
  local copies, waits for them, and re-layouts  0.66 us (2%)
  between operations  0.66 us (2%)
    pallas_call x1, Pallas kernels, per_device(): pl.pallas_call(functools.partial(kernel, gx_count, gy_count), out_shape=p...  34.6 us

profile of v4, /device:TPU:1, one launch (start us, length us, event | category | flops | bytes accessed | tf_op | source)
XLA Modules:
  0.0 35.9 jit_solution(16679522495349205602)
XLA Ops:
  0.7 34.6 %vcycle.1 = f32[2,128,128]{2,1,0:T(8,128)S(1)} custom-call(f32[2,128,128]{2,1,0:T(8,128)} %rhs_hbm.1, f32[128,128]{1,0:T(8,128)} %shift_hbm.1, f32[128,128]{1,0:T(8,128)} %visc_hbm.1, s32[1,1]{1,0:T(1,128)S(6)} %copy.7.wet_hbm), custom_call_target="tpu_custom_call" | custom-call | tf_op jit(solution)/shard_map/vcycle/pallas_call | solution.py:566
  35.2 0.7 %copy.6 = f32[2,128,128]{2,1,0:T(8,128)} copy(f32[2,128,128]{2,1,0:T(8,128)S(1)} %vcycle.1) | data formatting | bytes 262144
